TPU v7x, 32 devices: a whole 2x2x4 slice. The times are simulated.
32 devices in a mesh: loop: 4 (over y, x), bulk: 8 (over z, core).
Axes of the slice: x: 2, y: 2, z: 4, core: 2. Of those that a mesh axis runs over, the one named last changes fastest.
Arguments:
- series: float32 [4224, 3072], P('loop', 'bulk'), may hold values from -64 to 64
Outputs:
- correlation: float32 [4, 1056, 4224], P(None, 'bulk', 'loop')
All inputs are finite; a program needn't handle non-finite values.
Results may differ from a plain program's by a relative error of at most 0.0011.
Values may be sent and summed in bfloat16 or wider, within the bound.
A program may use at most 64 MiB of HBM per device.

v0:
```python
import functools
import jax
import jax.numpy as jnp
from jax import lax
from jax.experimental import pallas as pl
from jax.experimental.pallas import tpu as pltpu
from jax.sharding import PartitionSpec as P

epsilon = 1e-06
MESH = pl.DeviceIdType.MESH
NT = (((1,), (1,)), ((), ()))
TN = (((0,), (0,)), ((), ()))


def up_to(value, unit):
    return -(-value // unit) * unit


def largest_tile(rows, limit):
    return max(t for t in range(16, limit + 1, 16) if rows % t == 0)


def kernel(L, B, PIECES, x_hbm, o_ref, zbuf, shr, acc, cols, stats, x_ref,
           z_recv, up_send, down_send, mate_send, shr_recv, shr_send, st_recv, st_send, x_sem):
    R, T = x_hbm.shape
    total = T * B
    Q = B // 2
    share = R // B
    SP = shr.shape[2]
    W = min(up_to(share + 15, 16), R)
    bounds = [up_to(R * i // PIECES, 128) for i in range(PIECES)] + [R]
    tile = largest_tile(R, 128)
    l, b = lax.axis_index("loop"), lax.axis_index("bulk")
    q, c = b // 2, b % 2
    mate = q * 2 + (1 - c)

    barrier = pltpu.get_barrier_semaphore()
    for d in range(1, B):
        pl.semaphore_signal(barrier, inc=1, device_id=(l, lax.rem(b + d, B)), device_id_type=MESH)
    for d in range(1, L):
        pl.semaphore_signal(barrier, inc=1, device_id=(lax.rem(l + d, L), b), device_id_type=MESH)

    def load(i):
        rows = pl.ds(pl.multiple_of(i * tile, tile), tile)
        return pltpu.make_async_copy(x_hbm.at[rows, :], x_ref.at[rows, :], x_sem.at[i])

    @pl.loop(0, R // tile)
    def _(i):
        load(i).start()

    lane = lax.broadcasted_iota(jnp.int32, (tile, 128), 1)

    @pl.loop(0, R // tile)
    def _(i):
        rows = pl.ds(pl.multiple_of(i * tile, tile), tile)
        load(i).wait()
        v = x_ref[rows, :]
        mean = jnp.sum(v, axis=1, keepdims=True) / T
        dev = v - mean
        m2 = jnp.sum(dev * dev, axis=1, keepdims=True)
        cols[rows, :] = jnp.where(lane == 0, mean, jnp.where(lane == 1, m2, 0.0))

    pick = (lax.broadcasted_iota(jnp.int32, (8, 128), 0)
            == lax.broadcasted_iota(jnp.int32, (8, 128), 1)).astype(jnp.float32)
    line = lax.dot_general(pick, cols[...], NT, precision=lax.Precision.HIGHEST,
                           preferred_element_type=jnp.float32)
    stats[b] = line[:2]

    pl.semaphore_wait(barrier, B - 1 + L - 1)

    def stat_copy(source, peer):
        return pltpu.make_async_remote_copy(
            src_ref=stats.at[source], dst_ref=stats.at[source],
            send_sem=st_send.at[peer], recv_sem=st_recv.at[source],
            device_id=(l, peer), device_id_type=MESH)

    for d in range(1, B):
        stat_copy(b, lax.rem(b + d, B)).start()
    for d in range(1, B):
        other = lax.rem(b + d, B)
        stat_copy(other, other).wait_recv()

    mean = stats[0, 0:1]
    for k in range(1, B):
        mean = mean + stats[k, 0:1]
    mean = mean / B
    square = jnp.zeros_like(mean)
    for k in range(B):
        shift = stats[k, 0:1] - mean
        square = square + (stats[k, 1:2] + T * (shift * shift))
    scale = lax.rsqrt(square / total + epsilon)
    sub = lax.broadcasted_iota(jnp.int32, (8, R), 0)
    both = jnp.where(sub == 0, mean, jnp.where(sub == 1, scale, 0.0))
    cols[...] = lax.dot_general(both, pick, TN, precision=lax.Precision.HIGHEST,
                                preferred_element_type=jnp.float32)

    def normalise(piece):
        size = bounds[piece + 1] - bounds[piece]
        step = largest_tile(size, 128)

        @pl.loop(0, size // step)
        def _(i):
            rows = pl.ds(pl.multiple_of(bounds[piece] + i * step, 16), step)
            z = (x_ref[rows, :] - cols[rows, 0:1]) * cols[rows, 1:2]
            zbuf[b, rows, :] = z.astype(jnp.bfloat16)

    def piece_copy(k, piece, send_sem, peer):
        part = zbuf.at[k, pl.ds(bounds[piece], bounds[piece + 1] - bounds[piece]), :]
        return pltpu.make_async_remote_copy(
            src_ref=part, dst_ref=part, send_sem=send_sem.at[k, piece],
            recv_sem=z_recv.at[k, piece], device_id=(l, peer), device_id_type=MESH)

    def share_copy(k, block, peer):
        return pltpu.make_async_remote_copy(
            src_ref=shr.at[k, block], dst_ref=shr.at[k, block], send_sem=shr_send.at[k, peer],
            recv_sem=shr_recv.at[k, block], device_id=(peer, b), device_id_type=MESH)

    has_up, has_down = q + 1 < Q, q >= 1
    start = b * share
    first = pl.multiple_of(jnp.minimum(start // 16 * 16, R - W), 16)
    need_below = PIECES - 1 - sum((first >= x).astype(jnp.int32) for x in bounds[1:-1])
    need_above = sum((first + W > x).astype(jnp.int32) for x in bounds[1:-1])

    def extract(k):
        window = zbuf[k, pl.ds(first, W), :]
        hot = (lax.broadcasted_iota(jnp.int32, (SP, W), 1)
               == lax.broadcasted_iota(jnp.int32, (SP, W), 0) + (start - first))
        inside = lax.broadcasted_iota(jnp.int32, (SP, W), 0) < share
        hot = jnp.where(hot & inside, 1.0, 0.0).astype(jnp.bfloat16)
        rows = lax.dot_general(hot, window, (((1,), (0,)), ((), ())),
                               preferred_element_type=jnp.float32)
        shr[k, l] = rows.astype(jnp.bfloat16)
        for d in range(1, L):
            share_copy(k, l, lax.rem(l + d, L)).start()

    def wait_shares(place):
        for core in range(2):
            k = place * 2 + core
            for d in range(1, L):
                other = lax.rem(l + d, L)
                share_copy(k, other, other).wait_recv()

    def multiply(place):
        part = None
        wait_shares(place)
        for core in range(2):
            k = place * 2 + core
            a = shr[k].reshape(L * SP, T)
            term = lax.dot_general(a, zbuf[k], NT, preferred_element_type=jnp.float32)
            part = term if part is None else part + term
        acc[...] += part

    def multiply_step(s):
        @pl.loop(0, 2)
        def _(n):
            place = q - (1 - 2 * n) * s

            @pl.when((place >= 0) & (place < Q) & ((s > 0) | (n < 1)))
            def _():
                multiply(place)

    def send_own(up_first):
        done = set()

        def send(up, i):
            piece = PIECES - 1 - i if up else i
            if piece not in done:
                done.add(piece)
                normalise(piece)

            @pl.when(has_up if up else has_down)
            def _():
                if up:
                    piece_copy(b, piece, up_send, b + 2).start()
                else:
                    piece_copy(b, piece, down_send, b - 2).start()

        for i in range(PIECES):
            send(up_first, i)
            send(not up_first, i)

    @pl.when(q >= Q // 2)
    def _():
        send_own(True)

    @pl.when(q < Q // 2)
    def _():
        send_own(False)

    for i in range(PIECES):
        piece_copy(b, i, mate_send, mate).start()

    acc[...] = jnp.zeros_like(acc)
    extract(b)

    for i in range(PIECES):
        piece_copy(mate, i, mate_send, mate).wait_recv()

    extract(mate)

    def arrive(s, i, between=None):
        below, above = b - 2 * s, b + 2 * s
        from_below, from_above = q - s >= 0, q + s < Q
        down_piece = PIECES - 1 - i

        @pl.when(from_below)
        def _():
            piece_copy(below, down_piece, up_send, b).wait_recv()

            @pl.when(has_up)
            def _():
                piece_copy(below, down_piece, up_send, b + 2).start()
            piece_copy(below, down_piece, mate_send, mate).start()

        @pl.when(from_above)
        def _():
            piece_copy(above, i, down_send, b).wait_recv()

            @pl.when(has_down)
            def _():
                piece_copy(above, i, down_send, b - 2).start()
            piece_copy(above, i, mate_send, mate).start()

        @pl.when(from_below & (i == need_below))
        def _():
            extract(below)

        @pl.when(from_above & (i == need_above))
        def _():
            extract(above)

        if between is not None:
            between()

        @pl.when(from_below)
        def _():
            piece_copy(mate - 2 * s, down_piece, mate_send, mate).wait_recv()

            @pl.when(i == need_below)
            def _():
                extract(mate - 2 * s)

        @pl.when(from_above)
        def _():
            piece_copy(mate + 2 * s, i, mate_send, mate).wait_recv()

            @pl.when(i == need_above)
            def _():
                extract(mate + 2 * s)

        if i == 0:
            multiply_step(s - 1)

    def finish(piece, place):
        lo, hi = bounds[piece], bounds[piece + 1]
        part = acc[:, lo:hi]
        if place is not None:
            for core in range(2):
                k = place * 2 + core
                a = shr[k].reshape(L * SP, T)
                part = part + lax.dot_general(a, zbuf[k, lo:hi, :], NT,
                                              preferred_element_type=jnp.float32)
        part = part / total
        for j in range(L):
            o_ref[:, j, lo:hi] = part[j * SP:j * SP + share]

    @pl.loop(1, Q - 1)
    def _(s):
        for i in range(PIECES):
            arrive(s, i)

    def finish_ends(steps):
        for end, place in ((Q - 1, 0), (0, Q - 1)):
            @pl.when(q == end)
            def _():
                for i in steps:
                    finish(PIECES - 1 - i if end else i, place)

    def finish_early():
        for end, place in ((Q - 1, 0), (0, Q - 1)):
            @pl.when(q == end)
            def _():
                wait_shares(place)

        finish_ends(range(PIECES - 1))

    for i in range(PIECES):
        arrive(Q - 1, i, finish_early if i == PIECES - 1 else None)
    finish_ends([PIECES - 1])

    @pl.when((q > 0) & (q < Q - 1))
    def _():
        for i in range(PIECES):
            finish(i, None)

    for d in range(1, B):
        other = lax.rem(b + d, B)
        stat_copy(b, other).wait_send()

    @pl.loop(0, Q)
    def _(s):
        below, above = b - 2 * s, b + 2 * s
        from_below, from_above = q - s >= 0, q + s < Q

        for i in range(PIECES):
            @pl.when(from_below & has_up)
            def _():
                piece_copy(below, i, up_send, b + 2).wait_send()

            @pl.when(from_above & has_down)
            def _():
                piece_copy(above, i, down_send, b - 2).wait_send()

            @pl.when(from_below)
            def _():
                piece_copy(below, i, mate_send, mate).wait_send()

            @pl.when(from_above & (s > 0))
            def _():
                piece_copy(above, i, mate_send, mate).wait_send()

    @pl.loop(0, B)
    def _(k):
        for d in range(1, L):
            other = lax.rem(l + d, L)
            share_copy(k, l, other).wait_send()


def solution(mesh):
    L, B = mesh.shape["loop"], mesh.shape["bulk"]

    def on_device(series):
        R, T = series.shape
        share = R // B
        SP = up_to(share, 16)
        pieces = 3
        vmem = pl.BlockSpec(memory_space=pltpu.VMEM)
        dma = pltpu.SemaphoreType.DMA
        return pl.pallas_call(
            functools.partial(kernel, L, B, pieces),
            out_shape=jax.ShapeDtypeStruct((share, L, R), jnp.float32),
            in_specs=[pl.BlockSpec(memory_space=pltpu.HBM)],
            out_specs=vmem,
            scratch_shapes=[
                pltpu.VMEM((B, R, T), jnp.bfloat16),
                pltpu.VMEM((B, L, SP, T), jnp.bfloat16),
                pltpu.VMEM((L * SP, R), jnp.float32),
                pltpu.VMEM((R, 128), jnp.float32),
                pltpu.VMEM((B, 2, R), jnp.float32),
                pltpu.VMEM((R, T), jnp.float32),
                dma((B, pieces)), dma((B, pieces)), dma((B, pieces)), dma((B, pieces)),
                dma((B, L)), dma((B, L)), dma((B,)), dma((B,)), dma((R // largest_tile(R, 128),)),
            ],
            compiler_params=pltpu.CompilerParams(
                collective_id=0, has_side_effects=True, vmem_limit_bytes=26 * 1024 * 1024),
        )(pltpu.with_memory_space_constraint(series, pltpu.HBM)).transpose(1, 0, 2)

    return jax.shard_map(
        on_device, mesh=mesh, in_specs=(P("loop", "bulk"),),
        out_specs=P(None, "bulk", "loop"), check_vma=False)
```

profile of v0, /device:TPU:0, one launch (start us, length us, event | category | flops | bytes accessed | tf_op | source)
XLA Modules:
  0.0 71.4 jit_solution(7071849981405193399)
XLA Ops:
  0.0 70.0 %shard_map.17 = f32[132,4,1056]{2,1,0:T(4,128)S(1)} custom-call(f32[1056,384]{1,0:T(8,128)} %x_hbm.1), custom_call_target="tpu_custom_call" | custom-call | tf_op jit(solution)/shard_map/pallas_call | solution.py:339
  70.0 1.4 %copy.3 = f32[4,132,1056]{2,0,1:T(4,128)} copy(f32[4,132,1056]{2,0,1:T(4,128)S(1)} %bitcast.1) | data formatting | bytes 4460544
where the time goes:
time: 71.5 us; the launch traced here: 71.4 us
  Pallas kernels  70 us (98%)
  local copies, waits for them, and re-layouts  1.43 us (2%)
    pallas_call x1, Pallas kernels, on_device(): pl.pallas_call(functools.partial(kernel, L, B, pieces), out_shape=jax.Sha...  70 us
    unnamed x1, local copies, waits for them, and re-layouts  1.43 us

commit v1 on v0

--- a/solution.py
+++ b/solution.py
@@ -326,12 +326,459 @@
             share_copy(k, l, other).wait_send()
 
 
+D, S, A2, A1 = range(4)
+
+
+def line_kernel(L, B, x_hbm, o_ref, zbuf, shr, acc_t, acc_r, tile_send, tile_recv, cols, stats, x_ref,
+                z_recv, out_send, in_send, mate_send, shr_recv, shr_send, diag_recv, t_recv, t_send,
+                st_recv, st_send, x_sem):
+    R, T = x_hbm.shape
+    total = T * B
+    share = R // B
+    half = 2 * share
+    SP = shr.shape[2]
+    pad = share - 128
+    W = min(up_to(share + 15, 16), R)
+    skip_lo, skip_hi = up_to(R // 2 + pad, 16), (3 * half - pad) // 16 * 16
+    middle = up_to(skip_lo // 2, 16)
+    up_start = {D: skip_hi, S: skip_lo, A2: middle, A1: 0}
+    size = {D: R - skip_hi, S: skip_hi - skip_lo, A2: skip_lo - middle, A1: middle}
+    tile = largest_tile(R, 128)
+    NTL, NR = acc_t.shape[1], acc_r.shape[1]
+    l, b = lax.axis_index("loop"), lax.axis_index("bulk")
+    q, c = b // 2, b % 2
+    mate = q * 2 + (1 - c)
+    upper = q >= 2
+    inner = (q == 1) | (q == 2)
+    outer = (q == 0) | (q == 3)
+    step = jnp.where(upper, 1, -1)
+    H = [jnp.where(upper, h, 3 - h) for h in range(4)]
+    out_nbr, in_nbr = b + 2 * step, b - 2 * step
+    lx, ly, ld = l + 1 - 2 * (l % 2), lax.rem(l + 2, 4), 3 - l
+
+    def align(value, unit=16):
+        return pl.multiple_of(value, unit)
+
+    down_start = {p: R - up_start[p] - size[p] for p in up_start}
+    so = {p: align(jnp.where(upper, up_start[p], down_start[p])) for p in up_start}
+    si = {p: align(jnp.where(upper, down_start[p], up_start[p])) for p in up_start}
+    start_t = align(jnp.where(upper, R - NTL, 0), 128)
+    start_r = align(jnp.where(upper, 0, R - NR), 128)
+
+    barrier = pltpu.get_barrier_semaphore()
+    for d in range(1, B):
+        pl.semaphore_signal(barrier, inc=1, device_id=(l, lax.rem(b + d, B)), device_id_type=MESH)
+    facing = jnp.where(inner, H[3], H[2])
+    for d in range(1, L):
+        other = lax.rem(l + d, L)
+        pl.semaphore_signal(barrier, inc=1, device_id=(other, b), device_id_type=MESH)
+        for core in range(2):
+            pl.semaphore_signal(barrier, inc=1, device_id=(other, facing * 2 + core), device_id_type=MESH)
+
+    def load(i):
+        rows = pl.ds(pl.multiple_of(i * tile, tile), tile)
+        return pltpu.make_async_copy(x_hbm.at[rows, :], x_ref.at[rows, :], x_sem.at[i])
+
+    @pl.loop(0, R // tile)
+    def _(i):
+        load(i).start()
+
+    lane = lax.broadcasted_iota(jnp.int32, (tile, 128), 1)
+
+    @pl.loop(0, R // tile)
+    def _(i):
+        rows = pl.ds(pl.multiple_of(i * tile, tile), tile)
+        load(i).wait()
+        v = x_ref[rows, :]
+        mean = jnp.sum(v, axis=1, keepdims=True) / T
+        dev = v - mean
+        m2 = jnp.sum(dev * dev, axis=1, keepdims=True)
+        cols[rows, :] = jnp.where(lane == 0, mean, jnp.where(lane == 1, m2, 0.0))
+
+    pick = (lax.broadcasted_iota(jnp.int32, (8, 128), 0)
+            == lax.broadcasted_iota(jnp.int32, (8, 128), 1)).astype(jnp.float32)
+    line = lax.dot_general(pick, cols[...], NT, precision=lax.Precision.HIGHEST,
+                           preferred_element_type=jnp.float32)
+    stats[b] = line[:2]
+
+    pl.semaphore_wait(barrier, B - 1 + 3 * (L - 1))
+
+    def stat_copy(source, peer):
+        return pltpu.make_async_remote_copy(
+            src_ref=stats.at[source], dst_ref=stats.at[source],
+            send_sem=st_send.at[peer], recv_sem=st_recv.at[source],
+            device_id=(l, peer), device_id_type=MESH)
+
+    for d in range(1, B):
+        stat_copy(b, lax.rem(b + d, B)).start()
+    for d in range(1, B):
+        other = lax.rem(b + d, B)
+        stat_copy(other, other).wait_recv()
+
+    mean = stats[0, 0:1]
+    for k in range(1, B):
+        mean = mean + stats[k, 0:1]
+    mean = mean / B
+    square = jnp.zeros_like(mean)
+    for k in range(B):
+        shift = stats[k, 0:1] - mean
+        square = square + (stats[k, 1:2] + T * (shift * shift))
+    scale = lax.rsqrt(square / total + epsilon)
+    sub = lax.broadcasted_iota(jnp.int32, (8, R), 0)
+    both = jnp.where(sub == 0, mean, jnp.where(sub == 1, scale, 0.0))
+    cols[...] = lax.dot_general(both, pick, TN, precision=lax.Precision.HIGHEST,
+                                preferred_element_type=jnp.float32)
+
+    def normalise(start, rows_all):
+        unit = largest_tile(rows_all, 128)
+
+        @pl.loop(0, rows_all // unit)
+        def _(i):
+            rows = pl.ds(pl.multiple_of(start + i * unit, 16), unit)
+            z = (x_ref[rows, :] - cols[rows, 0:1]) * cols[rows, 1:2]
+            zbuf[b, rows, :] = z.astype(jnp.bfloat16)
+
+    def z_copy(k, start, p, send_sem, peer, rows=None):
+        part = zbuf.at[k, pl.ds(start, size[p] if rows is None else rows), :]
+        return pltpu.make_async_remote_copy(
+            src_ref=part, dst_ref=part, send_sem=send_sem.at[k, p],
+            recv_sem=z_recv.at[k, p], device_id=(l, peer), device_id_type=MESH)
+
+    def send_out(k, p):
+        return z_copy(k, so[p], p, out_send, out_nbr)
+
+    def send_in(k, p):
+        return z_copy(k, si[p], p, in_send, in_nbr)
+
+    def mate_copy(k, p, start):
+        return z_copy(k, start[p], p, mate_send, mate)
+
+    def mate_own(k):
+        return z_copy(k, 0, 0, mate_send, mate, R)
+
+    def share_copy(k, block, peer, way):
+        return pltpu.make_async_remote_copy(
+            src_ref=shr.at[k, block], dst_ref=shr.at[k, block], send_sem=shr_send.at[k, way],
+            recv_sem=shr_recv.at[k, way], device_id=(peer, b), device_id_type=MESH)
+
+    cut = up_to(SP // 2, 16)
+
+    def diag_copy(k, block, peer, way):
+        rows = pl.ds(0, cut) if way == 0 else pl.ds(cut, SP - cut)
+        part = shr.at[k, block, rows, :]
+        return pltpu.make_async_remote_copy(
+            src_ref=part, dst_ref=part, send_sem=shr_send.at[k, 2 + way],
+            recv_sem=diag_recv.at[k, way], device_id=(peer, b), device_id_type=MESH)
+
+    first = align(jnp.minimum(b * share // 16 * 16, jnp.where(q == 0, size[D], R) - W))
+
+    def extract(place):
+        @pl.loop(0, 2)
+        def _(core):
+            k = place * 2 + core
+            window = zbuf[k, pl.ds(first, W), :]
+            row = lax.broadcasted_iota(jnp.int32, (SP, W), 0)
+            hot = lax.broadcasted_iota(jnp.int32, (SP, W), 1) == row + (b * share - first)
+            hot = jnp.where(hot & (row < share), 1.0, 0.0).astype(jnp.bfloat16)
+            rows = lax.dot_general(hot, window, (((1,), (0,)), ((), ())),
+                                   preferred_element_type=jnp.float32)
+            shr[k, l] = rows.astype(jnp.bfloat16)
+            share_copy(k, l, lx, 0).start()
+            share_copy(k, l, ly, 1).start()
+
+    def pass_on(place):
+        @pl.loop(0, 2)
+        def _(core):
+            k = place * 2 + core
+            share_copy(k, lx, lx, 0).wait_recv()
+            diag_copy(k, lx, ly, 0).start()
+            share_copy(k, ly, ly, 1).wait_recv()
+            diag_copy(k, ly, lx, 1).start()
+
+    def wait_diag(place):
+        @pl.loop(0, 2)
+        def _(core):
+            k = place * 2 + core
+            for way in range(2):
+                diag_copy(k, ld, ld, way).wait_recv()
+
+    def product(place, start, width):
+        part = None
+        for core in range(2):
+            k = place * 2 + core
+            term = lax.dot_general(shr[k].reshape(L * SP, T), zbuf[k, pl.ds(start, width), :], NT,
+                                   preferred_element_type=jnp.float32)
+            part = term if part is None else part + term
+        return part
+
+    def own(h):
+        return H[h] * 2 + c
+
+    def other(h):
+        return H[h] * 2 + (1 - c)
+
+    def take(h, p, start, onward=None):
+        z_copy(own(h), start[p], p, mate_send, mate).wait_recv()
+        if onward is not None:
+            onward(own(h), p).start()
+        mate_copy(own(h), p, start).start()
+
+    def mate_take(h, pieces, start):
+        for p in pieces:
+            mate_copy(other(h), p, start).wait_recv()
+
+    normalise(so[D], size[D])
+
+    @pl.when(inner)
+    def _():
+        send_out(b, D).start()
+    normalise(align(jnp.where(upper, 0, size[D])), R - size[D])
+
+    @pl.when(inner)
+    def _():
+        for p in (D, S, A2):
+            send_in(b, p).start()
+        for p in (A2, A1):
+            send_out(b, p).start()
+
+    @pl.when(outer)
+    def _():
+        for p in (D, S, A2, A1):
+            send_in(b, p).start()
+    mate_own(b).start()
+    mate_own(mate).wait_recv()
+    extract(q)
+
+    @pl.when(inner)
+    def _():
+        take(1, D, so, send_out)
+        take(3, D, si, send_in)
+        pass_on(q)
+        take(1, S, so)
+        take(3, S, si, send_in)
+        take(1, A2, so, send_out)
+        take(3, A2, si, send_in)
+        send_in(b, A1).start()
+        mate_take(1, (D, S, A2), so)
+        extract(H[1])
+
+    @pl.when(outer)
+    def _():
+        take(2, D, so)
+        mate_take(2, (D,), so)
+        extract(H[2])
+        pass_on(q)
+        take(2, A2, so)
+        take(2, A1, so)
+        mate_take(2, (A2, A1), so)
+    wait_diag(q)
+    acc_t[...] = product(q, start_t, NTL)
+    acc_r[...] = product(q, start_r, NR)
+
+    @pl.when(inner)
+    def _():
+        take(0, D, so, send_out)
+        take(3, A1, si, send_in)
+        mate_take(3, (D, S, A2, A1), si)
+        extract(H[3])
+        pass_on(H[1])
+        take(0, S, so)
+        take(0, A2, so, send_out)
+        mate_take(0, (D, S, A2), so)
+        extract(H[0])
+        pass_on(H[3])
+
+    @pl.when(outer)
+    def _():
+        pass_on(H[2])
+        take(1, D, so)
+        mate_take(1, (D,), so)
+        extract(H[1])
+        take(1, A2, so)
+        pass_on(H[1])
+        take(0, D, so)
+        mate_take(0, (D,), so)
+        extract(H[0])
+    second, third = jnp.where(inner, H[1], H[2]), jnp.where(inner, H[3], H[1])
+    wait_diag(second)
+    acc_t[...] += product(second, start_t, NTL)
+
+    @pl.when(inner)
+    def _():
+        take(1, A1, so, send_out)
+        mate_take(1, (A1,), so)
+
+    @pl.when(outer)
+    def _():
+        take(0, A2, so)
+        pass_on(H[0])
+        take(1, A1, so)
+        mate_take(1, (A2, A1), so)
+    acc_r[...] += product(second, start_r, NR)
+    wait_diag(third)
+    acc_t[...] += product(third, start_t, NTL)
+    acc_r[...] += product(third, start_r, NR)
+
+    @pl.when(inner)
+    def _():
+        pass_on(H[0])
+        take(0, A1, so, send_out)
+
+    @pl.when(outer)
+    def _():
+        take(0, A1, so)
+        mate_take(0, (A2, A1), so)
+    wait_diag(H[0])
+    acc_t[...] += product(H[0], start_t, NTL)
+
+    def tile_copy(j, core, block, slot):
+        return pltpu.make_async_remote_copy(
+            src_ref=tile_send.at[j, pl.ds(core * SP, SP), :],
+            dst_ref=tile_recv.at[block, :, pl.ds(pl.multiple_of(slot * 128, 128), 128)],
+            send_sem=t_send.at[j, core], recv_sem=t_recv.at[block, slot],
+            device_id=(j, H[3] * 2 + core), device_id_type=MESH)
+
+    @pl.when(inner)
+    def _():
+        value = (acc_t[...] / total).astype(jnp.bfloat16)
+        row = lax.broadcasted_iota(jnp.int32, (2 * SP, NTL), 0)
+        lower = row < SP
+        want = jnp.where(lower, row, row - SP + share) + jnp.where(upper, NTL - half, 0)
+        keep = jnp.where(lower, row, row - SP) < share
+        hot = (lax.broadcasted_iota(jnp.int32, (2 * SP, NTL), 1) == want) & keep
+        hot = jnp.where(hot, 1.0, 0.0).astype(jnp.bfloat16)
+        picked = lax.dot_general(value, hot, NT, preferred_element_type=jnp.float32)
+        picked = picked.astype(jnp.bfloat16)
+        shift = (lax.broadcasted_iota(jnp.int32, (SP, 128), 0)
+                 == lax.broadcasted_iota(jnp.int32, (SP, 128), 1) + jnp.where(c == 0, pad, 0))
+        shift = jnp.where(shift, 1.0, 0.0).astype(jnp.bfloat16)
+        for j in range(L):
+            turned = lax.dot_general(picked[j * SP:(j + 1) * SP], shift, TN,
+                                     preferred_element_type=jnp.float32)
+            tile_send[j] = turned.astype(jnp.bfloat16)
+        for d in (1, 2, 3, 0):
+            for core in range(2):
+                tile_copy(lax.rem(l + d, L), core, l, c).start()
+        mate_take(0, (A1,), so)
+    acc_r[...] += product(H[0], start_r, NR)
+
+    def put(j, lo, hi, part):
+        o_ref[:, j, lo:hi] = part
+
+    def near(ref, j, lo, hi):
+        return ref[j * SP:j * SP + share, lo:hi] / total
+
+    t_lo, r_lo = R - NTL, R - NR
+    @pl.when(upper)
+    def _():
+        for j in range(L):
+            put(j, 0, t_lo, near(acc_r, j, 0, t_lo))
+            put(j, t_lo, R, near(acc_t, j, 0, NTL))
+
+    @pl.when(q < 2)
+    def _():
+        for j in range(L):
+            put(j, 0, r_lo, near(acc_t, j, 0, r_lo))
+            put(j, r_lo, R, near(acc_r, j, 0, NR))
+
+    @pl.when(outer)
+    def _():
+        from_up, from_down = R // 2 + pad, half + pad
+        base_up, base_down = from_up // 128 * 128, from_down // 128 * 128
+        width = up_to(max(from_up - base_up, from_down - base_down) + 256, 128)
+        offset = jnp.where(upper, from_up - base_up, from_down - base_down)
+        hot = (lax.broadcasted_iota(jnp.int32, (256, width), 1)
+               == lax.broadcasted_iota(jnp.int32, (256, width), 0) + offset)
+        hot = jnp.where(hot, 1.0, 0.0).astype(jnp.bfloat16)
+        place = lax.broadcasted_iota(jnp.int32, (share, width), 1)
+        inside = (place >= offset) & (place < offset + 256)
+        for d in range(L):
+            for slot in range(2):
+                tile_copy(l, 0, d, slot).wait_recv()
+            placed = lax.dot_general(tile_recv[d], hot, (((1,), (0,)), ((), ())),
+                                     preferred_element_type=jnp.float32)[:share]
+            for side, lo in ((3, base_up), (0, base_down)):
+                @pl.when(q == side)
+                def _():
+                    o_ref[:, d, lo:lo + width] = jnp.where(inside, placed, o_ref[:, d, lo:lo + width])
+
+    for d in range(1, B):
+        stat_copy(b, lax.rem(b + d, B)).wait_send()
+    mate_own(b).wait_send()
+
+    @pl.when(inner)
+    def _():
+        for h in (2, 1, 0):
+            for p in (D, A2, A1):
+                send_out(own(h), p).wait_send()
+        for h in (2, 3):
+            for p in (D, S, A2, A1):
+                send_in(own(h), p).wait_send()
+        for h, start in ((1, so), (0, so), (3, si)):
+            for p in (D, S, A2, A1):
+                mate_copy(own(h), p, start).wait_send()
+        for j in range(L):
+            for core in range(2):
+                tile_copy(j, core, l, c).wait_send()
+
+    @pl.when(outer)
+    def _():
+        for p in (D, S, A2, A1):
+            send_in(b, p).wait_send()
+        for h in (2, 1, 0):
+            for p in (D, A2, A1):
+                mate_copy(own(h), p, so).wait_send()
+
+    @pl.loop(0, B)
+    def _(k):
+        share_copy(k, l, lx, 0).wait_send()
+        share_copy(k, l, ly, 1).wait_send()
+        diag_copy(k, lx, ly, 0).wait_send()
+        diag_copy(k, ly, lx, 1).wait_send()
+
+
+def line_call(L, B, series):
+    R, T = series.shape
+    share = R // B
+    SP = up_to(share, 16)
+    pad = share - 128
+    skip_hi = (3 * 2 * share - pad) // 16 * 16
+    t_lo = skip_hi // 128 * 128
+    r_lo = (R - t_lo) // 128 * 128
+    vmem = pl.BlockSpec(memory_space=pltpu.VMEM)
+    dma = pltpu.SemaphoreType.DMA
+    return pl.pallas_call(
+        functools.partial(line_kernel, L, B),
+        out_shape=jax.ShapeDtypeStruct((share, L, R), jnp.float32),
+        in_specs=[pl.BlockSpec(memory_space=pltpu.HBM)],
+        out_specs=vmem,
+        scratch_shapes=[
+            pltpu.VMEM((B, R, T), jnp.bfloat16),
+            pltpu.VMEM((B, L, SP, T), jnp.bfloat16),
+            pltpu.VMEM((L * SP, R - t_lo), jnp.float32),
+            pltpu.VMEM((L * SP, R - r_lo), jnp.float32),
+            pltpu.VMEM((L, 2 * SP, 128), jnp.bfloat16),
+            pltpu.VMEM((L, SP, 256), jnp.bfloat16),
+            pltpu.VMEM((R, 128), jnp.float32),
+            pltpu.VMEM((B, 2, R), jnp.float32),
+            pltpu.VMEM((R, T), jnp.float32),
+            dma((B, 4)), dma((B, 4)), dma((B, 4)), dma((B, 4)),
+            dma((B, 2)), dma((B, 4)), dma((B, 2)), dma((L, 2)), dma((L, 2)),
+            dma((B,)), dma((B,)), dma((R // largest_tile(R, 128),)),
+        ],
+        compiler_params=pltpu.CompilerParams(
+            collective_id=0, has_side_effects=True, vmem_limit_bytes=34 * 1024 * 1024),
+    )(pltpu.with_memory_space_constraint(series, pltpu.HBM)).transpose(1, 0, 2)
+
+
 def solution(mesh):
     L, B = mesh.shape["loop"], mesh.shape["bulk"]
 
     def on_device(series):
         R, T = series.shape
         share = R // B
+        if L == 4 and B == 8 and R % 16 == 0 and T % 128 == 0 and 128 <= share <= 144:
+            return line_call(L, B, series)
         SP = up_to(share, 16)
         pieces = 3
         vmem = pl.BlockSpec(memory_space=pltpu.VMEM)

time: 71.5 us -> 71.9 us (level)
  no operation moved by 1% of the time
where the time goes in v1:
time: 71.9 us; the launch traced here: 71.8 us
  Pallas kernels  70.3 us (98%)
  local copies, waits for them, and re-layouts  1.43 us (2%)
    pallas_call x1, Pallas kernels, line_call(): pl.pallas_call(functools.partial(line_kernel, L, B), out_shape=jax.ShapeD...  70.3 us

profile of v1, /device:TPU:0, one launch (start us, length us, event | category | flops | bytes accessed | tf_op | source)
XLA Modules:
  0.0 71.8 jit_solution(1239856670691687406)
XLA Ops:
  0.0 70.3 %shard_map.17 = f32[132,4,1056]{2,1,0:T(4,128)S(1)} custom-call(f32[1056,384]{1,0:T(8,128)} %x_hbm.1), custom_call_target="tpu_custom_call" | custom-call | tf_op jit(solution)/shard_map/pallas_call | solution.py:750
  70.4 1.4 %copy.3 = f32[4,132,1056]{2,0,1:T(4,128)} copy(f32[4,132,1056]{2,0,1:T(4,128)S(1)} %bitcast.1) | data formatting | bytes 4460544

commit v2 on v1

--- a/solution.py
+++ b/solution.py
@@ -329,7 +329,7 @@
 D, S, A2, A1 = range(4)
 
 
-def line_kernel(L, B, x_hbm, o_ref, zbuf, shr, acc_t, acc_r, tile_send, tile_recv, cols, stats, x_ref,
+def line_kernel(L, B, x_hbm, o_ref, zbuf, shr, acc_t, acc_r, tile_send, tile_recv, hot_ref, shift_ref, cols, stats, x_ref,
                 z_recv, out_send, in_send, mate_send, shr_recv, shr_send, diag_recv, t_recv, t_send,
                 st_recv, st_send, x_sem):
     R, T = x_hbm.shape
@@ -429,14 +429,18 @@
     cols[...] = lax.dot_general(both, pick, TN, precision=lax.Precision.HIGHEST,
                                 preferred_element_type=jnp.float32)
 
-    def normalise(start, rows_all):
-        unit = largest_tile(rows_all, 128)
-
-        @pl.loop(0, rows_all // unit)
-        def _(i):
+    def normalise(start, count):
+        unit = count if count <= 288 else largest_tile(count, 128)
+
+        def chunk(i):
             rows = pl.ds(pl.multiple_of(start + i * unit, 16), unit)
             z = (x_ref[rows, :] - cols[rows, 0:1]) * cols[rows, 1:2]
             zbuf[b, rows, :] = z.astype(jnp.bfloat16)
+
+        if unit == count:
+            chunk(0)
+        else:
+            pl.loop(0, count // unit)(chunk)
 
     def z_copy(k, start, p, send_sem, peer, rows=None):
         part = zbuf.at[k, pl.ds(start, size[p] if rows is None else rows), :]
@@ -527,110 +531,6 @@
         for p in pieces:
             mate_copy(other(h), p, start).wait_recv()
 
-    normalise(so[D], size[D])
-
-    @pl.when(inner)
-    def _():
-        send_out(b, D).start()
-    normalise(align(jnp.where(upper, 0, size[D])), R - size[D])
-
-    @pl.when(inner)
-    def _():
-        for p in (D, S, A2):
-            send_in(b, p).start()
-        for p in (A2, A1):
-            send_out(b, p).start()
-
-    @pl.when(outer)
-    def _():
-        for p in (D, S, A2, A1):
-            send_in(b, p).start()
-    mate_own(b).start()
-    mate_own(mate).wait_recv()
-    extract(q)
-
-    @pl.when(inner)
-    def _():
-        take(1, D, so, send_out)
-        take(3, D, si, send_in)
-        pass_on(q)
-        take(1, S, so)
-        take(3, S, si, send_in)
-        take(1, A2, so, send_out)
-        take(3, A2, si, send_in)
-        send_in(b, A1).start()
-        mate_take(1, (D, S, A2), so)
-        extract(H[1])
-
-    @pl.when(outer)
-    def _():
-        take(2, D, so)
-        mate_take(2, (D,), so)
-        extract(H[2])
-        pass_on(q)
-        take(2, A2, so)
-        take(2, A1, so)
-        mate_take(2, (A2, A1), so)
-    wait_diag(q)
-    acc_t[...] = product(q, start_t, NTL)
-    acc_r[...] = product(q, start_r, NR)
-
-    @pl.when(inner)
-    def _():
-        take(0, D, so, send_out)
-        take(3, A1, si, send_in)
-        mate_take(3, (D, S, A2, A1), si)
-        extract(H[3])
-        pass_on(H[1])
-        take(0, S, so)
-        take(0, A2, so, send_out)
-        mate_take(0, (D, S, A2), so)
-        extract(H[0])
-        pass_on(H[3])
-
-    @pl.when(outer)
-    def _():
-        pass_on(H[2])
-        take(1, D, so)
-        mate_take(1, (D,), so)
-        extract(H[1])
-        take(1, A2, so)
-        pass_on(H[1])
-        take(0, D, so)
-        mate_take(0, (D,), so)
-        extract(H[0])
-    second, third = jnp.where(inner, H[1], H[2]), jnp.where(inner, H[3], H[1])
-    wait_diag(second)
-    acc_t[...] += product(second, start_t, NTL)
-
-    @pl.when(inner)
-    def _():
-        take(1, A1, so, send_out)
-        mate_take(1, (A1,), so)
-
-    @pl.when(outer)
-    def _():
-        take(0, A2, so)
-        pass_on(H[0])
-        take(1, A1, so)
-        mate_take(1, (A2, A1), so)
-    acc_r[...] += product(second, start_r, NR)
-    wait_diag(third)
-    acc_t[...] += product(third, start_t, NTL)
-    acc_r[...] += product(third, start_r, NR)
-
-    @pl.when(inner)
-    def _():
-        pass_on(H[0])
-        take(0, A1, so, send_out)
-
-    @pl.when(outer)
-    def _():
-        take(0, A1, so)
-        mate_take(0, (A2, A1), so)
-    wait_diag(H[0])
-    acc_t[...] += product(H[0], start_t, NTL)
-
     def tile_copy(j, core, block, slot):
         return pltpu.make_async_remote_copy(
             src_ref=tile_send.at[j, pl.ds(core * SP, SP), :],
@@ -638,28 +538,151 @@
             send_sem=t_send.at[j, core], recv_sem=t_recv.at[block, slot],
             device_id=(j, H[3] * 2 + core), device_id_type=MESH)
 
-    @pl.when(inner)
-    def _():
-        value = (acc_t[...] / total).astype(jnp.bfloat16)
+    def make_hot():
         row = lax.broadcasted_iota(jnp.int32, (2 * SP, NTL), 0)
         lower = row < SP
         want = jnp.where(lower, row, row - SP + share) + jnp.where(upper, NTL - half, 0)
         keep = jnp.where(lower, row, row - SP) < share
         hot = (lax.broadcasted_iota(jnp.int32, (2 * SP, NTL), 1) == want) & keep
-        hot = jnp.where(hot, 1.0, 0.0).astype(jnp.bfloat16)
-        picked = lax.dot_general(value, hot, NT, preferred_element_type=jnp.float32)
-        picked = picked.astype(jnp.bfloat16)
+        hot_ref[...] = jnp.where(hot, 1.0, 0.0).astype(jnp.bfloat16)
         shift = (lax.broadcasted_iota(jnp.int32, (SP, 128), 0)
                  == lax.broadcasted_iota(jnp.int32, (SP, 128), 1) + jnp.where(c == 0, pad, 0))
-        shift = jnp.where(shift, 1.0, 0.0).astype(jnp.bfloat16)
-        for j in range(L):
-            turned = lax.dot_general(picked[j * SP:(j + 1) * SP], shift, TN,
-                                     preferred_element_type=jnp.float32)
-            tile_send[j] = turned.astype(jnp.bfloat16)
-        for d in (1, 2, 3, 0):
-            for core in range(2):
-                tile_copy(lax.rem(l + d, L), core, l, c).start()
+        shift_ref[...] = jnp.where(shift, 1.0, 0.0).astype(jnp.bfloat16)
+
+    def finish_tile(j):
+        rows = pl.ds(pl.multiple_of(j * SP, SP), SP)
+        value = acc_t[rows, :]
+        for core in range(2):
+            k = H[0] * 2 + core
+            value = value + lax.dot_general(shr[k, j], zbuf[k, pl.ds(start_t, NTL), :], NT,
+                                            preferred_element_type=jnp.float32)
+        acc_t[rows, :] = value
+        turned = lax.dot_general((value / total).astype(jnp.bfloat16), shift_ref[...], TN,
+                                 preferred_element_type=jnp.float32)
+        picked = lax.dot_general(hot_ref[...], turned.astype(jnp.bfloat16), (((1,), (0,)), ((), ())),
+                                 preferred_element_type=jnp.float32)
+        tile_send[j] = picked.astype(jnp.bfloat16)
+        for core in range(2):
+            tile_copy(j, core, l, c).start()
+
+    normalise(so[D], size[D])
+
+    @pl.when(inner)
+    def _():
+        send_out(b, D).start()
+    normalise(align(jnp.where(upper, 0, size[D])), R - size[D])
+
+    @pl.when(inner)
+    def _():
+        for p in (D, S, A2):
+            send_in(b, p).start()
+        for p in (A2, A1):
+            send_out(b, p).start()
+
+    @pl.when(outer)
+    def _():
+        for p in (A2, A1, D, S):
+            send_in(b, p).start()
+    mate_own(b).start()
+    make_hot()
+    mate_own(mate).wait_recv()
+    extract(q)
+
+    @pl.when(inner)
+    def _():
+        take(1, D, so, send_out)
+        take(3, A2, si, send_in)
+        pass_on(q)
+        take(1, S, so)
+        take(3, A1, si)
+        mate_take(3, (A2, A1), si)
+        extract(H[3])
+        take(1, A2, so, send_out)
+        take(3, D, si, send_in)
+        mate_take(1, (D, S, A2), so)
+        extract(H[1])
+
+    @pl.when(outer)
+    def _():
+        take(2, D, so)
+        mate_take(2, (D,), so)
+        extract(H[2])
+        pass_on(q)
+        take(2, A2, so)
+        pass_on(H[2])
+        take(2, A1, so)
+        mate_take(2, (A2, A1), so)
+    wait_diag(q)
+    acc_t[...] = product(q, start_t, NTL)
+    acc_r[...] = product(q, start_r, NR)
+
+    second, third = jnp.where(inner, H[3], H[2]), H[1]
+
+    @pl.when(inner)
+    def _():
+        pass_on(H[3])
+        take(0, A2, so, send_out)
+        take(3, S, si, send_in)
+        send_in(b, A1).start()
+        send_in(own(3), A1).start()
+        mate_take(3, (D, S), si)
+        pass_on(H[1])
+        take(0, D, so, send_out)
+
+    @pl.when(outer)
+    def _():
+        take(1, D, so)
+        mate_take(1, (D,), so)
+        extract(H[1])
+    wait_diag(second)
+    acc_t[...] += product(second, start_t, NTL)
+    acc_r[...] += product(second, start_r, NR)
+
+    @pl.when(inner)
+    def _():
+        take(0, S, so)
+        mate_take(0, (A2, D, S), so)
+        extract(H[0])
+
+    @pl.when(outer)
+    def _():
+        take(1, A2, so)
+        pass_on(H[1])
+        take(0, A2, so)
+        take(0, D, so)
+        mate_take(0, (D,), so)
+        extract(H[0])
+        take(1, A1, so)
+        mate_take(1, (A2, A1), so)
+    wait_diag(third)
+    acc_t[...] += product(third, start_t, NTL)
+
+    @pl.when(inner)
+    def _():
+        finish_tile(l)
+        take(1, A1, so, send_out)
+        mate_take(1, (A1,), so)
+    acc_r[...] += product(third, start_r, NR)
+
+    @pl.when(inner)
+    def _():
+        pass_on(H[0])
+
+        @pl.loop(0, 2)
+        def _(n):
+            finish_tile(jnp.where(n == 0, lx, ly))
+        take(0, A1, so, send_out)
+        wait_diag(H[0])
+        finish_tile(ld)
         mate_take(0, (A1,), so)
+
+    @pl.when(outer)
+    def _():
+        pass_on(H[0])
+        take(0, A1, so)
+        mate_take(0, (A2, A1), so)
+        wait_diag(H[0])
+        acc_t[...] += product(H[0], start_t, NTL)
     acc_r[...] += product(H[0], start_r, NR)
 
     def put(j, lo, hi, part):
@@ -692,7 +715,7 @@
         hot = jnp.where(hot, 1.0, 0.0).astype(jnp.bfloat16)
         place = lax.broadcasted_iota(jnp.int32, (share, width), 1)
         inside = (place >= offset) & (place < offset + 256)
-        for d in range(L):
+        for d in (l, lx, ly, ld):
             for slot in range(2):
                 tile_copy(l, 0, d, slot).wait_recv()
             placed = lax.dot_general(tile_recv[d], hot, (((1,), (0,)), ((), ())),
@@ -759,6 +782,8 @@
             pltpu.VMEM((L * SP, R - r_lo), jnp.float32),
             pltpu.VMEM((L, 2 * SP, 128), jnp.bfloat16),
             pltpu.VMEM((L, SP, 256), jnp.bfloat16),
+            pltpu.VMEM((2 * SP, R - t_lo), jnp.bfloat16),
+            pltpu.VMEM((SP, 128), jnp.bfloat16),
             pltpu.VMEM((R, 128), jnp.float32),
             pltpu.VMEM((B, 2, R), jnp.float32),
             pltpu.VMEM((R, T), jnp.float32),

time: 71.9 us -> 68.6 us (0.954); the launches traced: 71.8 us -> 67.5 us
  Pallas kernels: 70.3 us -> 66.1 us
    pallas_call x1, Pallas kernels: 70.3 us -> 66.1 us  [line_call(): pl.pallas_call(functools.partial(line_kernel, L, B), out_shape=jax.ShapeD...]
where the time goes in v2:
time: 68.6 us; the launch traced here: 67.5 us
  Pallas kernels  66.1 us (96%)
  local copies, waits for them, and re-layouts  1.43 us (2%)
    pallas_call x1, Pallas kernels, line_call(): pl.pallas_call(functools.partial(line_kernel, L, B), out_shape=jax.ShapeD...  66.1 us
    unnamed x1, local copies, waits for them, and re-layouts  1.43 us

profile of v2, /device:TPU:0, one launch (start us, length us, event | category | flops | bytes accessed | tf_op | source)
XLA Modules:
  0.0 67.5 jit_solution(15959484506852851357)
XLA Ops:
  0.0 66.1 %shard_map.17 = f32[132,4,1056]{2,1,0:T(4,128)S(1)} custom-call(f32[1056,384]{1,0:T(8,128)} %x_hbm.1), custom_call_target="tpu_custom_call" | custom-call | tf_op jit(solution)/shard_map/pallas_call | solution.py:773
  66.1 1.4 %copy.3 = f32[4,132,1056]{2,0,1:T(4,128)} copy(f32[4,132,1056]{2,0,1:T(4,128)S(1)} %bitcast.1) | data formatting | bytes 4460544

commit v3 on v2

--- a/solution.py
+++ b/solution.py
@@ -330,7 +330,7 @@
 
 
 def line_kernel(L, B, x_hbm, o_ref, zbuf, shr, acc_t, acc_r, tile_send, tile_recv, hot_ref, shift_ref, cols, stats, x_ref,
-                z_recv, out_send, in_send, mate_send, shr_recv, shr_send, diag_recv, t_recv, t_send,
+                z_recv, out_send, in_send, mate_send, own_send, shr_recv, shr_send, diag_recv, diag_send, t_recv, t_send,
                 st_recv, st_send, x_sem):
     R, T = x_hbm.shape
     total = T * B
@@ -343,7 +343,7 @@
     middle = up_to(skip_lo // 2, 16)
     up_start = {D: skip_hi, S: skip_lo, A2: middle, A1: 0}
     size = {D: R - skip_hi, S: skip_hi - skip_lo, A2: skip_lo - middle, A1: middle}
-    tile = largest_tile(R, 128)
+    tile = largest_tile(R, 352)
     NTL, NR = acc_t.shape[1], acc_r.shape[1]
     l, b = lax.axis_index("loop"), lax.axis_index("bulk")
     q, c = b // 2, b % 2
@@ -406,14 +406,16 @@
     def stat_copy(source, peer):
         return pltpu.make_async_remote_copy(
             src_ref=stats.at[source], dst_ref=stats.at[source],
-            send_sem=st_send.at[peer], recv_sem=st_recv.at[source],
+            send_sem=st_send, recv_sem=st_recv,
             device_id=(l, peer), device_id_type=MESH)
 
     for d in range(1, B):
         stat_copy(b, lax.rem(b + d, B)).start()
-    for d in range(1, B):
-        other = lax.rem(b + d, B)
-        stat_copy(other, other).wait_recv()
+    gathered = stats.at[pl.ds(0, B - 1)]
+    all_stats = pltpu.make_async_remote_copy(
+        src_ref=gathered, dst_ref=gathered, send_sem=st_send, recv_sem=st_recv,
+        device_id=(l, b), device_id_type=MESH)
+    all_stats.wait_recv()
 
     mean = stats[0, 0:1]
     for k in range(1, B):
@@ -445,7 +447,7 @@
     def z_copy(k, start, p, send_sem, peer, rows=None):
         part = zbuf.at[k, pl.ds(start, size[p] if rows is None else rows), :]
         return pltpu.make_async_remote_copy(
-            src_ref=part, dst_ref=part, send_sem=send_sem.at[k, p],
+            src_ref=part, dst_ref=part, send_sem=send_sem,
             recv_sem=z_recv.at[k, p], device_id=(l, peer), device_id_type=MESH)
 
     def send_out(k, p):
@@ -458,11 +460,11 @@
         return z_copy(k, start[p], p, mate_send, mate)
 
     def mate_own(k):
-        return z_copy(k, 0, 0, mate_send, mate, R)
+        return z_copy(k, 0, 0, own_send, mate, R)
 
     def share_copy(k, block, peer, way):
         return pltpu.make_async_remote_copy(
-            src_ref=shr.at[k, block], dst_ref=shr.at[k, block], send_sem=shr_send.at[k, way],
+            src_ref=shr.at[k, block], dst_ref=shr.at[k, block], send_sem=shr_send,
             recv_sem=shr_recv.at[k, way], device_id=(peer, b), device_id_type=MESH)
 
     cut = up_to(SP // 2, 16)
@@ -471,8 +473,8 @@
         rows = pl.ds(0, cut) if way == 0 else pl.ds(cut, SP - cut)
         part = shr.at[k, block, rows, :]
         return pltpu.make_async_remote_copy(
-            src_ref=part, dst_ref=part, send_sem=shr_send.at[k, 2 + way],
-            recv_sem=diag_recv.at[k, way], device_id=(peer, b), device_id_type=MESH)
+            src_ref=part, dst_ref=part, send_sem=diag_send,
+            recv_sem=diag_recv.at[k // 2], device_id=(peer, b), device_id_type=MESH)
 
     first = align(jnp.minimum(b * share // 16 * 16, jnp.where(q == 0, size[D], R) - W))
 
@@ -500,11 +502,10 @@
             diag_copy(k, ly, lx, 1).start()
 
     def wait_diag(place):
-        @pl.loop(0, 2)
-        def _(core):
-            k = place * 2 + core
-            for way in range(2):
-                diag_copy(k, ld, ld, way).wait_recv()
+        part = shr.at[pl.ds(place * 2, 2), ld]
+        pltpu.make_async_remote_copy(
+            src_ref=part, dst_ref=part, send_sem=diag_send, recv_sem=diag_recv.at[place],
+            device_id=(l, b), device_id_type=MESH).wait_recv()
 
     def product(place, start, width):
         part = None
@@ -535,7 +536,7 @@
         return pltpu.make_async_remote_copy(
             src_ref=tile_send.at[j, pl.ds(core * SP, SP), :],
             dst_ref=tile_recv.at[block, :, pl.ds(pl.multiple_of(slot * 128, 128), 128)],
-            send_sem=t_send.at[j, core], recv_sem=t_recv.at[block, slot],
+            send_sem=t_send, recv_sem=t_recv.at[block],
             device_id=(j, H[3] * 2 + core), device_id_type=MESH)
 
     def make_hot():
@@ -562,8 +563,16 @@
         picked = lax.dot_general(hot_ref[...], turned.astype(jnp.bfloat16), (((1,), (0,)), ((), ())),
                                  preferred_element_type=jnp.float32)
         tile_send[j] = picked.astype(jnp.bfloat16)
+
+    def start_tile(j):
         for core in range(2):
             tile_copy(j, core, l, c).start()
+
+    def wait_tile(block):
+        part = tile_recv.at[block]
+        pltpu.make_async_remote_copy(
+            src_ref=part, dst_ref=part, send_sem=t_send, recv_sem=t_recv.at[block],
+            device_id=(l, b), device_id_type=MESH).wait_recv()
 
     normalise(so[D], size[D])
 
@@ -652,6 +661,7 @@
         take(0, D, so)
         mate_take(0, (D,), so)
         extract(H[0])
+        pass_on(H[0])
         take(1, A1, so)
         mate_take(1, (A2, A1), so)
     wait_diag(third)
@@ -672,17 +682,19 @@
         def _(n):
             finish_tile(jnp.where(n == 0, lx, ly))
         take(0, A1, so, send_out)
+        for j in (lx, ly, l):
+            start_tile(j)
         wait_diag(H[0])
         finish_tile(ld)
+        start_tile(ld)
         mate_take(0, (A1,), so)
 
     @pl.when(outer)
     def _():
-        pass_on(H[0])
+        wait_diag(H[0])
+        acc_t[...] += product(H[0], start_t, NTL)
         take(0, A1, so)
         mate_take(0, (A2, A1), so)
-        wait_diag(H[0])
-        acc_t[...] += product(H[0], start_t, NTL)
     acc_r[...] += product(H[0], start_r, NR)
 
     def put(j, lo, hi, part):
@@ -716,8 +728,7 @@
         place = lax.broadcasted_iota(jnp.int32, (share, width), 1)
         inside = (place >= offset) & (place < offset + 256)
         for d in (l, lx, ly, ld):
-            for slot in range(2):
-                tile_copy(l, 0, d, slot).wait_recv()
+            wait_tile(d)
             placed = lax.dot_general(tile_recv[d], hot, (((1,), (0,)), ((), ())),
                                      preferred_element_type=jnp.float32)[:share]
             for side, lo in ((3, base_up), (0, base_down)):
@@ -725,39 +736,30 @@
                 def _():
                     o_ref[:, d, lo:lo + width] = jnp.where(inside, placed, o_ref[:, d, lo:lo + width])
 
-    for d in range(1, B):
-        stat_copy(b, lax.rem(b + d, B)).wait_send()
+    all_stats.wait_send()
     mate_own(b).wait_send()
 
+    def sent(part, sem):
+        pltpu.make_async_remote_copy(
+            src_ref=part, dst_ref=part, send_sem=sem, recv_sem=st_recv,
+            device_id=(l, b), device_id_type=MESH).wait_send()
+
+    near_end = R - size[S]
+
     @pl.when(inner)
     def _():
-        for h in (2, 1, 0):
-            for p in (D, A2, A1):
-                send_out(own(h), p).wait_send()
-        for h in (2, 3):
-            for p in (D, S, A2, A1):
-                send_in(own(h), p).wait_send()
-        for h, start in ((1, so), (0, so), (3, si)):
-            for p in (D, S, A2, A1):
-                mate_copy(own(h), p, start).wait_send()
-        for j in range(L):
-            for core in range(2):
-                tile_copy(j, core, l, c).wait_send()
+        sent(zbuf.at[pl.ds(0, 3), pl.ds(0, near_end), :], out_send)
+        sent(zbuf.at[pl.ds(0, 2)], in_send)
+        sent(zbuf.at[pl.ds(0, 3)], mate_send)
+        sent(tile_send, t_send)
 
     @pl.when(outer)
     def _():
-        for p in (D, S, A2, A1):
-            send_in(b, p).wait_send()
-        for h in (2, 1, 0):
-            for p in (D, A2, A1):
-                mate_copy(own(h), p, so).wait_send()
-
-    @pl.loop(0, B)
-    def _(k):
-        share_copy(k, l, lx, 0).wait_send()
-        share_copy(k, l, ly, 1).wait_send()
-        diag_copy(k, lx, ly, 0).wait_send()
-        diag_copy(k, ly, lx, 1).wait_send()
+        sent(zbuf.at[pl.ds(0, 1)], in_send)
+        sent(zbuf.at[pl.ds(0, 3), pl.ds(0, near_end), :], mate_send)
+
+    sent(shr.at[pl.ds(0, L)], shr_send)
+    sent(shr.at[pl.ds(0, B // L)], diag_send)
 
 
 def line_call(L, B, series):
@@ -787,9 +789,9 @@
             pltpu.VMEM((R, 128), jnp.float32),
             pltpu.VMEM((B, 2, R), jnp.float32),
             pltpu.VMEM((R, T), jnp.float32),
-            dma((B, 4)), dma((B, 4)), dma((B, 4)), dma((B, 4)),
-            dma((B, 2)), dma((B, 4)), dma((B, 2)), dma((L, 2)), dma((L, 2)),
-            dma((B,)), dma((B,)), dma((R // largest_tile(R, 128),)),
+            dma((B, 4)), dma, dma, dma, dma,
+            dma((B, 2)), dma, dma((B // 2,)), dma, dma((L,)), dma,
+            dma, dma, dma((R // largest_tile(R, 352),)),
         ],
         compiler_params=pltpu.CompilerParams(
             collective_id=0, has_side_effects=True, vmem_limit_bytes=34 * 1024 * 1024),

time: 68.6 us -> 64.4 us (0.939); the launches traced: 67.5 us -> 64.3 us
  Pallas kernels: 66.1 us -> 62.8 us
    pallas_call x1, Pallas kernels: 66.1 us -> 62.8 us  [line_call(): pl.pallas_call(functools.partial(line_kernel, L, B), out_shape=jax.ShapeD...]
where the time goes in v3:
time: 64.4 us; the launch traced here: 64.3 us
  Pallas kernels  62.8 us (98%)
  local copies, waits for them, and re-layouts  1.43 us (2%)
    pallas_call x1, Pallas kernels, line_call(): pl.pallas_call(functools.partial(line_kernel, L, B), out_shape=jax.ShapeD...  62.8 us
    unnamed x1, local copies, waits for them, and re-layouts  1.43 us

profile of v3, /device:TPU:0, one launch (start us, length us, event | category | flops | bytes accessed | tf_op | source)
XLA Modules:
  0.0 64.3 jit_solution(1575571792823381859)
XLA Ops:
  0.0 62.8 %shard_map.17 = f32[132,4,1056]{2,1,0:T(4,128)S(1)} custom-call(f32[1056,384]{1,0:T(8,128)} %x_hbm.1), custom_call_target="tpu_custom_call" | custom-call | tf_op jit(solution)/shard_map/pallas_call | solution.py:775
  62.8 1.4 %copy.3 = f32[4,132,1056]{2,0,1:T(4,128)} copy(f32[4,132,1056]{2,0,1:T(4,128)S(1)} %bitcast.1) | data formatting | bytes 4460544

commit v4 on v3

--- a/solution.py
+++ b/solution.py
@@ -329,8 +329,8 @@
 D, S, A2, A1 = range(4)
 
 
-def line_kernel(L, B, x_hbm, o_ref, zbuf, shr, acc_t, acc_r, tile_send, tile_recv, hot_ref, shift_ref, cols, stats, x_ref,
-                z_recv, out_send, in_send, mate_send, own_send, shr_recv, shr_send, diag_recv, diag_send, t_recv, t_send,
+def line_kernel(L, B, x_hbm, o_ref, zbuf, shr, acc_t, acc_r, tile_send, tile_recv, hot_ref, shift_ref, cols, stats, x_ref, raw,
+                z_recv, out_send, in_send, mate_send, own_send, own_out, own_in, first_send, raw_recv, raw_send, shr_recv, shr_send, diag_recv, diag_send, t_recv, t_send,
                 st_recv, st_send, x_sem):
     R, T = x_hbm.shape
     total = T * B
@@ -344,6 +344,7 @@
     up_start = {D: skip_hi, S: skip_lo, A2: middle, A1: 0}
     size = {D: R - skip_hi, S: skip_hi - skip_lo, A2: skip_lo - middle, A1: middle}
     tile = largest_tile(R, 352)
+    RAW = raw.shape[1]
     NTL, NR = acc_t.shape[1], acc_r.shape[1]
     l, b = lax.axis_index("loop"), lax.axis_index("bulk")
     q, c = b // 2, b % 2
@@ -411,6 +412,20 @@
 
     for d in range(1, B):
         stat_copy(b, lax.rem(b + d, B)).start()
+    def raw_copy(start, slot, peer):
+        return pltpu.make_async_remote_copy(
+            src_ref=x_ref.at[pl.ds(start, RAW), :], dst_ref=raw.at[slot], send_sem=raw_send,
+            recv_sem=raw_recv.at[slot], device_id=(l, peer), device_id_type=MESH)
+
+    @pl.when(inner)
+    def _():
+        raw_copy(so[D], 0, out_nbr).start()
+        raw_copy(si[D], 0, in_nbr).start()
+
+    @pl.when(outer)
+    def _():
+        raw_copy(si[A2], 1, in_nbr).start()
+
     gathered = stats.at[pl.ds(0, B - 1)]
     all_stats = pltpu.make_async_remote_copy(
         src_ref=gathered, dst_ref=gathered, send_sem=st_send, recv_sem=st_recv,
@@ -450,6 +465,15 @@
             src_ref=part, dst_ref=part, send_sem=send_sem,
             recv_sem=z_recv.at[k, p], device_id=(l, peer), device_id_type=MESH)
 
+    def first_copy(k, p, start, peer):
+        return z_copy(k, align(start[p] + RAW), p, first_send, peer, size[p] - RAW)
+
+    def unpack(slot, k, start):
+        raw_copy(start, slot, b).wait_recv()
+        rows = pl.ds(start, RAW)
+        z = (raw[slot] - cols[rows, 0:1]) * cols[rows, 1:2]
+        zbuf[k, rows, :] = z.astype(jnp.bfloat16)
+
     def send_out(k, p):
         return z_copy(k, so[p], p, out_send, out_nbr)
 
@@ -522,8 +546,11 @@
     def other(h):
         return H[h] * 2 + (1 - c)
 
-    def take(h, p, start, onward=None):
-        z_copy(own(h), start[p], p, mate_send, mate).wait_recv()
+    def take(h, p, start, onward=None, first=False):
+        if first:
+            first_copy(own(h), p, start, mate).wait_recv()
+        else:
+            z_copy(own(h), start[p], p, mate_send, mate).wait_recv()
         if onward is not None:
             onward(own(h), p).start()
         mate_copy(own(h), p, start).start()
@@ -578,20 +605,22 @@
 
     @pl.when(inner)
     def _():
-        send_out(b, D).start()
+        first_copy(b, D, so, out_nbr).start()
     normalise(align(jnp.where(upper, 0, size[D])), R - size[D])
 
     @pl.when(inner)
     def _():
-        for p in (D, S, A2):
-            send_in(b, p).start()
+        first_copy(b, D, si, in_nbr).start()
+        for p in (S, A2):
+            z_copy(b, si[p], p, own_in, in_nbr).start()
         for p in (A2, A1):
-            send_out(b, p).start()
+            z_copy(b, so[p], p, own_out, out_nbr).start()
 
     @pl.when(outer)
     def _():
-        for p in (A2, A1, D, S):
-            send_in(b, p).start()
+        first_copy(b, A2, si, in_nbr).start()
+        for p in (A1, D, S):
+            z_copy(b, si[p], p, own_in, in_nbr).start()
     mate_own(b).start()
     make_hot()
     mate_own(mate).wait_recv()
@@ -599,8 +628,10 @@
 
     @pl.when(inner)
     def _():
-        take(1, D, so, send_out)
-        take(3, A2, si, send_in)
+        unpack(0, own(1), so[D])
+        unpack(1, own(3), si[A2])
+        take(1, D, so, send_out, True)
+        take(3, A2, si, send_in, True)
         pass_on(q)
         take(1, S, so)
         take(3, A1, si)
@@ -613,7 +644,8 @@
 
     @pl.when(outer)
     def _():
-        take(2, D, so)
+        unpack(0, own(2), so[D])
+        take(2, D, so, None, True)
         mate_take(2, (D,), so)
         extract(H[2])
         pass_on(q)
@@ -632,7 +664,7 @@
         pass_on(H[3])
         take(0, A2, so, send_out)
         take(3, S, si, send_in)
-        send_in(b, A1).start()
+        z_copy(b, si[A1], A1, own_in, in_nbr).start()
         send_in(own(3), A1).start()
         mate_take(3, (D, S), si)
         pass_on(H[1])
@@ -671,6 +703,7 @@
     def _():
         finish_tile(l)
         take(1, A1, so, send_out)
+        start_tile(l)
         mate_take(1, (A1,), so)
     acc_r[...] += product(third, start_r, NR)
 
@@ -682,7 +715,7 @@
         def _(n):
             finish_tile(jnp.where(n == 0, lx, ly))
         take(0, A1, so, send_out)
-        for j in (lx, ly, l):
+        for j in (lx, ly):
             start_tile(j)
         wait_diag(H[0])
         finish_tile(ld)
@@ -748,14 +781,20 @@
 
     @pl.when(inner)
     def _():
-        sent(zbuf.at[pl.ds(0, 3), pl.ds(0, near_end), :], out_send)
-        sent(zbuf.at[pl.ds(0, 2)], in_send)
+        sent(zbuf.at[0, pl.ds(0, size[A2] + size[A1]), :], own_out)
+        sent(zbuf.at[0, pl.ds(0, R - size[D]), :], own_in)
+        sent(zbuf.at[pl.ds(0, 2), pl.ds(0, size[D] - RAW), :], first_send)
+        sent(raw, raw_send)
+        sent(zbuf.at[pl.ds(0, 2), pl.ds(0, near_end), :], out_send)
+        sent(zbuf.at[pl.ds(0, 1)], in_send)
         sent(zbuf.at[pl.ds(0, 3)], mate_send)
         sent(tile_send, t_send)
 
     @pl.when(outer)
     def _():
-        sent(zbuf.at[pl.ds(0, 1)], in_send)
+        sent(zbuf.at[0, pl.ds(0, R - size[A2]), :], own_in)
+        sent(zbuf.at[0, pl.ds(0, size[A2] - RAW), :], first_send)
+        sent(raw.at[0], raw_send)
         sent(zbuf.at[pl.ds(0, 3), pl.ds(0, near_end), :], mate_send)
 
     sent(shr.at[pl.ds(0, L)], shr_send)
@@ -789,7 +828,8 @@
             pltpu.VMEM((R, 128), jnp.float32),
             pltpu.VMEM((B, 2, R), jnp.float32),
             pltpu.VMEM((R, T), jnp.float32),
-            dma((B, 4)), dma, dma, dma, dma,
+            pltpu.VMEM((2, (R - skip_hi) // 32 * 16, T), jnp.float32),
+            dma((B, 4)), dma, dma, dma, dma, dma, dma, dma, dma((2,)), dma,
             dma((B, 2)), dma, dma((B // 2,)), dma, dma((L,)), dma,
             dma, dma, dma((R // largest_tile(R, 352),)),
         ],

time: 64.4 us -> 61.8 us (0.960)
  Pallas kernels: 62.8 us -> 60.3 us
    pallas_call x1, Pallas kernels: 62.8 us -> 60.3 us  [line_call(): pl.pallas_call(functools.partial(line_kernel, L, B), out_shape=jax.ShapeD...]
where the time goes in v4:
time: 61.8 us; the launch traced here: 61.7 us
  Pallas kernels  60.3 us (98%)
  local copies, waits for them, and re-layouts  1.43 us (2%)
    pallas_call x1, Pallas kernels, line_call(): pl.pallas_call(functools.partial(line_kernel, L, B), out_shape=jax.ShapeD...  60.3 us
    unnamed x1, local copies, waits for them, and re-layouts  1.43 us

profile of v4, /device:TPU:0, one launch (start us, length us, event | category | flops | bytes accessed | tf_op | source)
XLA Modules:
  0.0 61.7 jit_solution(2854694631257766833)
XLA Ops:
  0.0 60.3 %shard_map.17 = f32[132,4,1056]{2,1,0:T(4,128)S(1)} custom-call(f32[1056,384]{1,0:T(8,128)} %x_hbm.1), custom_call_target="tpu_custom_call" | custom-call | tf_op jit(solution)/shard_map/pallas_call | solution.py:814
  60.3 1.4 %copy.3 = f32[4,132,1056]{2,0,1:T(4,128)} copy(f32[4,132,1056]{2,0,1:T(4,128)S(1)} %bitcast.1) | data formatting | bytes 4460544

commit v5 on v3

--- a/solution.py
+++ b/solution.py
@@ -326,11 +326,12 @@
             share_copy(k, l, other).wait_send()
 
 
-D, S, A2, A1 = range(4)
-
-
-def line_kernel(L, B, x_hbm, o_ref, zbuf, shr, acc_t, acc_r, tile_send, tile_recv, hot_ref, shift_ref, cols, stats, x_ref,
-                z_recv, out_send, in_send, mate_send, own_send, shr_recv, shr_send, diag_recv, diag_send, t_recv, t_send,
+F, M, C, N, D = range(5)
+
+
+def line_kernel(L, B, x_hbm, o_ref, zbuf, shr, acc_lo, acc_hi, acc_mid, tile_send, tile_recv, shift_ref, place_ref,
+                cols, stats, x_ref, raw,
+                z_recv, out_send, in_send, mate_send, own_send, own_out, own_in, first_send, raw_recv, raw_send, shr_recv, shr_send, diag_recv, diag_send, t_recv, t_send,
                 st_recv, st_send, x_sem):
     R, T = x_hbm.shape
     total = T * B
@@ -339,12 +340,15 @@
     SP = shr.shape[2]
     pad = share - 128
     W = min(up_to(share + 15, 16), R)
-    skip_lo, skip_hi = up_to(R // 2 + pad, 16), (3 * half - pad) // 16 * 16
-    middle = up_to(skip_lo // 2, 16)
-    up_start = {D: skip_hi, S: skip_lo, A2: middle, A1: 0}
-    size = {D: R - skip_hi, S: skip_hi - skip_lo, A2: skip_lo - middle, A1: middle}
+    low, high = R - (3 * half - pad) // 16 * 16, (3 * half - pad) // 16 * 16
+    edges = [0, low, (R // 2 - pad) // 16 * 16, up_to(R // 2 + pad, 16), high, R]
+    size = [edges[p + 1] - edges[p] for p in range(5)]
+    far = size[F] + size[C] + size[D]
     tile = largest_tile(R, 352)
-    NTL, NR = acc_t.shape[1], acc_r.shape[1]
+    RAW = raw.shape[1]
+    WS = acc_lo.shape[1]
+    hi_lane, mid_lane = R - WS, WS // 128 * 128
+    WM = acc_mid.shape[1]
     l, b = lax.axis_index("loop"), lax.axis_index("bulk")
     q, c = b // 2, b % 2
     mate = q * 2 + (1 - c)
@@ -359,21 +363,19 @@
     def align(value, unit=16):
         return pl.multiple_of(value, unit)
 
-    down_start = {p: R - up_start[p] - size[p] for p in up_start}
-    so = {p: align(jnp.where(upper, up_start[p], down_start[p])) for p in up_start}
-    si = {p: align(jnp.where(upper, down_start[p], up_start[p])) for p in up_start}
-    start_t = align(jnp.where(upper, R - NTL, 0), 128)
-    start_r = align(jnp.where(upper, 0, R - NR), 128)
+    start = [align(jnp.where(upper, edges[p], edges[4 - p])) for p in range(5)]
 
     barrier = pltpu.get_barrier_semaphore()
     for d in range(1, B):
         pl.semaphore_signal(barrier, inc=1, device_id=(l, lax.rem(b + d, B)), device_id_type=MESH)
-    facing = jnp.where(inner, H[3], H[2])
+    facing = [jnp.where(inner, 3 * side, 1 + side) for side in range(2)]
     for d in range(1, L):
         other = lax.rem(l + d, L)
         pl.semaphore_signal(barrier, inc=1, device_id=(other, b), device_id_type=MESH)
-        for core in range(2):
-            pl.semaphore_signal(barrier, inc=1, device_id=(other, facing * 2 + core), device_id_type=MESH)
+        for side in range(2):
+            for core in range(2):
+                pl.semaphore_signal(barrier, inc=1, device_id=(other, facing[side] * 2 + core),
+                                    device_id_type=MESH)
 
     def load(i):
         rows = pl.ds(pl.multiple_of(i * tile, tile), tile)
@@ -401,7 +403,7 @@
                            preferred_element_type=jnp.float32)
     stats[b] = line[:2]
 
-    pl.semaphore_wait(barrier, B - 1 + 3 * (L - 1))
+    pl.semaphore_wait(barrier, B - 1 + 5 * (L - 1))
 
     def stat_copy(source, peer):
         return pltpu.make_async_remote_copy(
@@ -411,6 +413,20 @@
 
     for d in range(1, B):
         stat_copy(b, lax.rem(b + d, B)).start()
+    def raw_copy(p, slot, peer):
+        return pltpu.make_async_remote_copy(
+            src_ref=x_ref.at[pl.ds(start[p], RAW), :], dst_ref=raw.at[slot], send_sem=raw_send,
+            recv_sem=raw_recv.at[slot], device_id=(l, peer), device_id_type=MESH)
+
+    @pl.when(inner)
+    def _():
+        raw_copy(D, 0, out_nbr).start()
+        raw_copy(F, 0, in_nbr).start()
+
+    @pl.when(outer)
+    def _():
+        raw_copy(D, 1, in_nbr).start()
+
     gathered = stats.at[pl.ds(0, B - 1)]
     all_stats = pltpu.make_async_remote_copy(
         src_ref=gathered, dst_ref=gathered, send_sem=st_send, recv_sem=st_recv,
@@ -431,11 +447,11 @@
     cols[...] = lax.dot_general(both, pick, TN, precision=lax.Precision.HIGHEST,
                                 preferred_element_type=jnp.float32)
 
-    def normalise(start, count):
+    def normalise(begin, count):
         unit = count if count <= 288 else largest_tile(count, 128)
 
         def chunk(i):
-            rows = pl.ds(pl.multiple_of(start + i * unit, 16), unit)
+            rows = pl.ds(pl.multiple_of(begin + i * unit, 16), unit)
             z = (x_ref[rows, :] - cols[rows, 0:1]) * cols[rows, 1:2]
             zbuf[b, rows, :] = z.astype(jnp.bfloat16)
 
@@ -444,23 +460,35 @@
         else:
             pl.loop(0, count // unit)(chunk)
 
-    def z_copy(k, start, p, send_sem, peer, rows=None):
-        part = zbuf.at[k, pl.ds(start, size[p] if rows is None else rows), :]
+    def z_copy(k, p, send_sem, peer, skip=0):
+        part = zbuf.at[k, pl.ds(align(start[p] + skip), size[p] - skip), :]
         return pltpu.make_async_remote_copy(
             src_ref=part, dst_ref=part, send_sem=send_sem,
-            recv_sem=z_recv.at[k, p], device_id=(l, peer), device_id_type=MESH)
+            recv_sem=z_recv.at[k, jnp.where(upper, p, 4 - p)], device_id=(l, peer), device_id_type=MESH)
+
+    def first_copy(k, p, peer):
+        return z_copy(k, p, first_send, peer, RAW)
+
+    def unpack(slot, k):
+        raw_copy(D, slot, b).wait_recv()
+        rows = pl.ds(start[D], RAW)
+        z = (raw[slot] - cols[rows, 0:1]) * cols[rows, 1:2]
+        zbuf[k, rows, :] = z.astype(jnp.bfloat16)
 
     def send_out(k, p):
-        return z_copy(k, so[p], p, out_send, out_nbr)
+        return z_copy(k, p, out_send, out_nbr)
 
     def send_in(k, p):
-        return z_copy(k, si[p], p, in_send, in_nbr)
-
-    def mate_copy(k, p, start):
-        return z_copy(k, start[p], p, mate_send, mate)
+        return z_copy(k, p, in_send, in_nbr)
+
+    def mate_copy(k, p):
+        return z_copy(k, p, mate_send, mate)
 
     def mate_own(k):
-        return z_copy(k, 0, 0, own_send, mate, R)
+        part = zbuf.at[k]
+        return pltpu.make_async_remote_copy(
+            src_ref=part, dst_ref=part, send_sem=own_send, recv_sem=z_recv.at[k, 0],
+            device_id=(l, mate), device_id_type=MESH)
 
     def share_copy(k, block, peer, way):
         return pltpu.make_async_remote_copy(
@@ -507,66 +535,76 @@
             src_ref=part, dst_ref=part, send_sem=diag_send, recv_sem=diag_recv.at[place],
             device_id=(l, b), device_id_type=MESH).wait_recv()
 
-    def product(place, start, width):
+    def product(place, begin, width):
         part = None
         for core in range(2):
             k = place * 2 + core
-            term = lax.dot_general(shr[k].reshape(L * SP, T), zbuf[k, pl.ds(start, width), :], NT,
+            term = lax.dot_general(shr[k].reshape(L * SP, T), zbuf[k, begin:begin + width, :], NT,
                                    preferred_element_type=jnp.float32)
             part = term if part is None else part + term
         return part
 
+    def add_sides(place):
+        acc_lo[...] += product(place, 0, WS)
+        acc_hi[...] += product(place, hi_lane, WS)
+
+    def add_middle(place):
+        acc_mid[...] += product(place, mid_lane, WM)
+
     def own(h):
         return H[h] * 2 + c
 
     def other(h):
         return H[h] * 2 + (1 - c)
 
-    def take(h, p, start, onward=None):
-        z_copy(own(h), start[p], p, mate_send, mate).wait_recv()
+    def take(h, p, onward=None, first=False):
+        if first:
+            first_copy(own(h), p, mate).wait_recv()
+        else:
+            mate_copy(own(h), p).wait_recv()
         if onward is not None:
             onward(own(h), p).start()
-        mate_copy(own(h), p, start).start()
-
-    def mate_take(h, pieces, start):
+        mate_copy(own(h), p).start()
+
+    def mate_take(h, pieces):
         for p in pieces:
-            mate_copy(other(h), p, start).wait_recv()
-
-    def tile_copy(j, core, block, slot):
-        return pltpu.make_async_remote_copy(
-            src_ref=tile_send.at[j, pl.ds(core * SP, SP), :],
+            mate_copy(other(h), p).wait_recv()
+
+    def tile_copy(side, j, core, block, slot):
+        return pltpu.make_async_remote_copy(
+            src_ref=tile_send.at[side, j, pl.ds(core * SP, SP), :],
             dst_ref=tile_recv.at[block, :, pl.ds(pl.multiple_of(slot * 128, 128), 128)],
             send_sem=t_send, recv_sem=t_recv.at[block],
-            device_id=(j, H[3] * 2 + core), device_id_type=MESH)
+            device_id=(j, 6 * side + core), device_id_type=MESH)
 
     def make_hot():
-        row = lax.broadcasted_iota(jnp.int32, (2 * SP, NTL), 0)
-        lower = row < SP
-        want = jnp.where(lower, row, row - SP + share) + jnp.where(upper, NTL - half, 0)
-        keep = jnp.where(lower, row, row - SP) < share
-        hot = (lax.broadcasted_iota(jnp.int32, (2 * SP, NTL), 1) == want) & keep
-        hot_ref[...] = jnp.where(hot, 1.0, 0.0).astype(jnp.bfloat16)
         shift = (lax.broadcasted_iota(jnp.int32, (SP, 128), 0)
                  == lax.broadcasted_iota(jnp.int32, (SP, 128), 1) + jnp.where(c == 0, pad, 0))
         shift_ref[...] = jnp.where(shift, 1.0, 0.0).astype(jnp.bfloat16)
-
-    def finish_tile(j):
+        row = lax.broadcasted_iota(jnp.int32, (512, WM), 0)
+        lane = jnp.where(row < 256, row + half + pad, row - 256 + R // 2 + pad) - mid_lane
+        hot = lax.broadcasted_iota(jnp.int32, (512, WM), 1) == lane
+        place_ref[...] = jnp.where(hot, 1.0, 0.0).astype(jnp.bfloat16)
+
+    def finish_tiles(j):
         rows = pl.ds(pl.multiple_of(j * SP, SP), SP)
-        value = acc_t[rows, :]
-        for core in range(2):
-            k = H[0] * 2 + core
-            value = value + lax.dot_general(shr[k, j], zbuf[k, pl.ds(start_t, NTL), :], NT,
-                                            preferred_element_type=jnp.float32)
-        acc_t[rows, :] = value
-        turned = lax.dot_general((value / total).astype(jnp.bfloat16), shift_ref[...], TN,
-                                 preferred_element_type=jnp.float32)
-        picked = lax.dot_general(hot_ref[...], turned.astype(jnp.bfloat16), (((1,), (0,)), ((), ())),
-                                 preferred_element_type=jnp.float32)
-        tile_send[j] = picked.astype(jnp.bfloat16)
-
-    def start_tile(j):
-        for core in range(2):
-            tile_copy(j, core, l, c).start()
+        for side, acc, begin in ((0, acc_lo, 0), (1, acc_hi, hi_lane)):
+            value = acc[rows, :]
+            for core in range(2):
+                k = H[0] * 2 + core
+                value = value + lax.dot_general(shr[k, j], zbuf[k, begin:begin + WS, :], NT,
+                                                preferred_element_type=jnp.float32)
+            acc[rows, :] = value
+            turned = lax.dot_general((value / total).astype(jnp.bfloat16), shift_ref[...], TN,
+                                     preferred_element_type=jnp.float32)
+            for core in range(2):
+                at = (WS - half if side else 0) + core * share
+                tile_send[side, j, core * SP:core * SP + share, :] = turned[at:at + share].astype(jnp.bfloat16)
+
+    def start_tiles(j):
+        for side in range(2):
+            for core in range(2):
+                tile_copy(side, j, core, l, b - 2).start()
 
     def wait_tile(block):
         part = tile_recv.at[block]
@@ -574,24 +612,33 @@
             src_ref=part, dst_ref=part, send_sem=t_send, recv_sem=t_recv.at[block],
             device_id=(l, b), device_id_type=MESH).wait_recv()
 
-    normalise(so[D], size[D])
-
-    @pl.when(inner)
-    def _():
-        send_out(b, D).start()
-    normalise(align(jnp.where(upper, 0, size[D])), R - size[D])
-
-    @pl.when(inner)
-    def _():
-        for p in (D, S, A2):
-            send_in(b, p).start()
-        for p in (A2, A1):
-            send_out(b, p).start()
+    normalise(start[D], size[D])
+
+    @pl.when(inner)
+    def _():
+        first_copy(b, D, out_nbr).start()
 
     @pl.when(outer)
     def _():
-        for p in (A2, A1, D, S):
-            send_in(b, p).start()
+        first_copy(b, D, in_nbr).start()
+    normalise(start[F], size[F])
+
+    @pl.when(inner)
+    def _():
+        first_copy(b, F, in_nbr).start()
+    normalise(low, high - low)
+
+    @pl.when(inner)
+    def _():
+        for p in (M, C, D):
+            z_copy(b, p, own_in, in_nbr).start()
+        for p in (F, C):
+            z_copy(b, p, own_out, out_nbr).start()
+
+    @pl.when(outer)
+    def _():
+        for p in (N, C, F, M):
+            z_copy(b, p, own_in, in_nbr).start()
     mate_own(b).start()
     make_hot()
     mate_own(mate).wait_recv()
@@ -599,142 +646,133 @@
 
     @pl.when(inner)
     def _():
-        take(1, D, so, send_out)
-        take(3, A2, si, send_in)
+        unpack(0, own(1))
+        unpack(1, own(3))
+        take(1, D, send_out, True)
+        take(3, D, None, True)
         pass_on(q)
-        take(1, S, so)
-        take(3, A1, si)
-        mate_take(3, (A2, A1), si)
+        take(1, N)
+        take(3, N)
+        take(1, C, send_out)
+        take(3, C)
+        mate_take(3, (D, N, C))
         extract(H[3])
-        take(1, A2, so, send_out)
-        take(3, D, si, send_in)
-        mate_take(1, (D, S, A2), so)
+        mate_take(1, (D, N, C))
         extract(H[1])
 
     @pl.when(outer)
     def _():
-        take(2, D, so)
-        mate_take(2, (D,), so)
+        unpack(0, own(2))
+        take(2, D, None, True)
+        mate_take(2, (D,))
         extract(H[2])
         pass_on(q)
-        take(2, A2, so)
+        take(2, F)
+        take(2, C)
+        mate_take(2, (F, C))
+    wait_diag(q)
+    acc_lo[...] = product(q, 0, WS)
+    acc_hi[...] = product(q, hi_lane, WS)
+    acc_mid[...] = product(q, mid_lane, WM)
+
+    second, third = jnp.where(inner, H[3], H[2]), H[1]
+
+    @pl.when(inner)
+    def _():
+        take(1, F, send_out)
+        take(3, F, send_in)
+        send_in(own(3), C).start()
+        pass_on(H[3])
+        take(3, M, send_in)
+        send_in(own(3), D).start()
+        take(0, D, send_out)
+        take(0, C, send_out)
+        pass_on(H[1])
+        take(0, N)
+        mate_take(3, (F, M))
+        mate_take(0, (D, C, N))
+        extract(H[0])
+
+    @pl.when(outer)
+    def _():
         pass_on(H[2])
-        take(2, A1, so)
-        mate_take(2, (A2, A1), so)
-    wait_diag(q)
-    acc_t[...] = product(q, start_t, NTL)
-    acc_r[...] = product(q, start_r, NR)
-
-    second, third = jnp.where(inner, H[3], H[2]), H[1]
-
-    @pl.when(inner)
-    def _():
-        pass_on(H[3])
-        take(0, A2, so, send_out)
-        take(3, S, si, send_in)
-        send_in(b, A1).start()
-        send_in(own(3), A1).start()
-        mate_take(3, (D, S), si)
+        take(1, D)
+        mate_take(1, (D,))
+        extract(H[1])
+        take(1, C)
+    wait_diag(second)
+    add_sides(second)
+    add_middle(second)
+
+    @pl.when(inner)
+    def _():
+        take(0, F, send_out)
+        z_copy(b, N, own_in, in_nbr).start()
+        mate_take(1, (F,))
+        mate_take(0, (F,))
+
+    @pl.when(outer)
+    def _():
+        take(1, F)
         pass_on(H[1])
-        take(0, D, so, send_out)
-
-    @pl.when(outer)
-    def _():
-        take(1, D, so)
-        mate_take(1, (D,), so)
-        extract(H[1])
-    wait_diag(second)
-    acc_t[...] += product(second, start_t, NTL)
-    acc_r[...] += product(second, start_r, NR)
-
-    @pl.when(inner)
-    def _():
-        take(0, S, so)
-        mate_take(0, (A2, D, S), so)
+        take(0, D)
+        mate_take(0, (D,))
         extract(H[0])
-
-    @pl.when(outer)
-    def _():
-        take(1, A2, so)
-        pass_on(H[1])
-        take(0, A2, so)
-        take(0, D, so)
-        mate_take(0, (D,), so)
-        extract(H[0])
-        pass_on(H[0])
-        take(1, A1, so)
-        mate_take(1, (A2, A1), so)
+        take(0, C)
+        mate_take(1, (C, F))
     wait_diag(third)
-    acc_t[...] += product(third, start_t, NTL)
-
-    @pl.when(inner)
-    def _():
-        finish_tile(l)
-        take(1, A1, so, send_out)
-        mate_take(1, (A1,), so)
-    acc_r[...] += product(third, start_r, NR)
-
-    @pl.when(inner)
-    def _():
-        pass_on(H[0])
+    add_sides(third)
+
+    pass_on(H[0])
+
+    @pl.when(inner)
+    def _():
+        finish_tiles(l)
+        start_tiles(l)
 
         @pl.loop(0, 2)
         def _(n):
-            finish_tile(jnp.where(n == 0, lx, ly))
-        take(0, A1, so, send_out)
-        for j in (lx, ly, l):
-            start_tile(j)
+            j = jnp.where(n == 0, lx, ly)
+            finish_tiles(j)
+            start_tiles(j)
+        send_in(own(3), N).start()
+        take(1, M)
         wait_diag(H[0])
-        finish_tile(ld)
-        start_tile(ld)
-        mate_take(0, (A1,), so)
+        finish_tiles(ld)
+        start_tiles(ld)
+        mate_take(1, (M,))
+    add_middle(third)
+
+    @pl.when(inner)
+    def _():
+        take(0, M)
+        mate_take(0, (M,))
 
     @pl.when(outer)
     def _():
+        take(0, F)
+        mate_take(0, (C, F))
         wait_diag(H[0])
-        acc_t[...] += product(H[0], start_t, NTL)
-        take(0, A1, so)
-        mate_take(0, (A2, A1), so)
-    acc_r[...] += product(H[0], start_r, NR)
-
-    def put(j, lo, hi, part):
-        o_ref[:, j, lo:hi] = part
-
-    def near(ref, j, lo, hi):
-        return ref[j * SP:j * SP + share, lo:hi] / total
-
-    t_lo, r_lo = R - NTL, R - NR
-    @pl.when(upper)
-    def _():
-        for j in range(L):
-            put(j, 0, t_lo, near(acc_r, j, 0, t_lo))
-            put(j, t_lo, R, near(acc_t, j, 0, NTL))
-
-    @pl.when(q < 2)
-    def _():
-        for j in range(L):
-            put(j, 0, r_lo, near(acc_t, j, 0, r_lo))
-            put(j, r_lo, R, near(acc_r, j, 0, NR))
+        add_sides(H[0])
+    add_middle(H[0])
+
+    for j in range(L):
+        rows = slice(j * SP, j * SP + share)
+        o_ref[:, j, :mid_lane] = acc_lo[rows, :mid_lane] / total
+        o_ref[:, j, mid_lane:mid_lane + WM] = acc_mid[rows, :] / total
+        o_ref[:, j, mid_lane + WM:] = acc_hi[rows, :][:, mid_lane + WM - hi_lane:] / total
 
     @pl.when(outer)
     def _():
-        from_up, from_down = R // 2 + pad, half + pad
-        base_up, base_down = from_up // 128 * 128, from_down // 128 * 128
-        width = up_to(max(from_up - base_up, from_down - base_down) + 256, 128)
-        offset = jnp.where(upper, from_up - base_up, from_down - base_down)
-        hot = (lax.broadcasted_iota(jnp.int32, (256, width), 1)
-               == lax.broadcasted_iota(jnp.int32, (256, width), 0) + offset)
-        hot = jnp.where(hot, 1.0, 0.0).astype(jnp.bfloat16)
-        place = lax.broadcasted_iota(jnp.int32, (share, width), 1)
-        inside = (place >= offset) & (place < offset + 256)
+        place = lax.broadcasted_iota(jnp.int32, (share, WM), 1) + mid_lane
+        inside = ((place >= half + pad) & (place < half + pad + 256)
+                  | (place >= R // 2 + pad) & (place < R // 2 + pad + 256))
         for d in (l, lx, ly, ld):
             wait_tile(d)
-            placed = lax.dot_general(tile_recv[d], hot, (((1,), (0,)), ((), ())),
+            placed = lax.dot_general(tile_recv[d], place_ref[...], (((1,), (0,)), ((), ())),
                                      preferred_element_type=jnp.float32)[:share]
-            for side, lo in ((3, base_up), (0, base_down)):
-                @pl.when(q == side)
-                def _():
-                    o_ref[:, d, lo:lo + width] = jnp.where(inside, placed, o_ref[:, d, lo:lo + width])
+            middle = pl.ds(mid_lane, WM)
+            o_ref[:, d, middle] = jnp.where(inside, placed, o_ref[:, d, middle])
 
     all_stats.wait_send()
     mate_own(b).wait_send()
@@ -744,20 +782,23 @@
             src_ref=part, dst_ref=part, send_sem=sem, recv_sem=st_recv,
             device_id=(l, b), device_id_type=MESH).wait_send()
 
-    near_end = R - size[S]
-
-    @pl.when(inner)
-    def _():
-        sent(zbuf.at[pl.ds(0, 3), pl.ds(0, near_end), :], out_send)
-        sent(zbuf.at[pl.ds(0, 2)], in_send)
+    @pl.when(inner)
+    def _():
+        sent(zbuf.at[0, pl.ds(0, size[F] + size[C]), :], own_out)
+        sent(zbuf.at[pl.ds(0, 2), pl.ds(0, size[D] - RAW), :], first_send)
+        sent(raw, raw_send)
+        sent(zbuf.at[pl.ds(0, 2), pl.ds(0, far), :], out_send)
+        sent(zbuf.at[0], in_send)
         sent(zbuf.at[pl.ds(0, 3)], mate_send)
         sent(tile_send, t_send)
 
     @pl.when(outer)
     def _():
-        sent(zbuf.at[pl.ds(0, 1)], in_send)
-        sent(zbuf.at[pl.ds(0, 3), pl.ds(0, near_end), :], mate_send)
-
+        sent(zbuf.at[0, pl.ds(0, size[D] - RAW), :], first_send)
+        sent(raw.at[0], raw_send)
+        sent(zbuf.at[pl.ds(0, 3), pl.ds(0, far), :], mate_send)
+
+    sent(zbuf.at[0, pl.ds(0, R - size[D]), :], own_in)
     sent(shr.at[pl.ds(0, L)], shr_send)
     sent(shr.at[pl.ds(0, B // L)], diag_send)
 
@@ -767,9 +808,10 @@
     share = R // B
     SP = up_to(share, 16)
     pad = share - 128
-    skip_hi = (3 * 2 * share - pad) // 16 * 16
-    t_lo = skip_hi // 128 * 128
-    r_lo = (R - t_lo) // 128 * 128
+    high = (3 * 2 * share - pad) // 16 * 16
+    WS = R - high
+    mid_lane = WS // 128 * 128
+    WM = up_to(R // 2 + pad + 256, 128) - mid_lane
     vmem = pl.BlockSpec(memory_space=pltpu.VMEM)
     dma = pltpu.SemaphoreType.DMA
     return pl.pallas_call(
@@ -780,16 +822,18 @@
         scratch_shapes=[
             pltpu.VMEM((B, R, T), jnp.bfloat16),
             pltpu.VMEM((B, L, SP, T), jnp.bfloat16),
-            pltpu.VMEM((L * SP, R - t_lo), jnp.float32),
-            pltpu.VMEM((L * SP, R - r_lo), jnp.float32),
-            pltpu.VMEM((L, 2 * SP, 128), jnp.bfloat16),
-            pltpu.VMEM((L, SP, 256), jnp.bfloat16),
-            pltpu.VMEM((2 * SP, R - t_lo), jnp.bfloat16),
+            pltpu.VMEM((L * SP, WS), jnp.float32),
+            pltpu.VMEM((L * SP, WS), jnp.float32),
+            pltpu.VMEM((L * SP, WM), jnp.float32),
+            pltpu.VMEM((2, L, 2 * SP, 128), jnp.bfloat16),
+            pltpu.VMEM((L, SP, 512), jnp.bfloat16),
             pltpu.VMEM((SP, 128), jnp.bfloat16),
+            pltpu.VMEM((512, WM), jnp.bfloat16),
             pltpu.VMEM((R, 128), jnp.float32),
             pltpu.VMEM((B, 2, R), jnp.float32),
             pltpu.VMEM((R, T), jnp.float32),
-            dma((B, 4)), dma, dma, dma, dma,
+            pltpu.VMEM((2, (R - high) // 32 * 16, T), jnp.float32),
+            dma((B, 5)), dma, dma, dma, dma, dma, dma, dma, dma((2,)), dma,
             dma((B, 2)), dma, dma((B // 2,)), dma, dma((L,)), dma,
             dma, dma, dma((R // largest_tile(R, 352),)),
         ],

time: 64.4 us -> 63.6 us (0.988)
  Pallas kernels: 62.8 us -> 62 us
    pallas_call x1, Pallas kernels: 62.8 us -> 62 us  [line_call(): pl.pallas_call(functools.partial(line_kernel, L, B), out_shape=jax.ShapeD...]
where the time goes in v5:
time: 63.6 us; the launch traced here: 63.5 us
  Pallas kernels  62 us (97%)
  local copies, waits for them, and re-layouts  1.43 us (2%)
    pallas_call x1, Pallas kernels, line_call(): pl.pallas_call(functools.partial(line_kernel, L, B), out_shape=jax.ShapeD...  62 us
    unnamed x1, local copies, waits for them, and re-layouts  1.43 us

profile of v5, /device:TPU:0, one launch (start us, length us, event | category | flops | bytes accessed | tf_op | source)
XLA Modules:
  0.0 63.5 jit_solution(10464620011596480658)
XLA Ops:
  0.0 62.0 %shard_map.17 = f32[132,4,1056]{2,1,0:T(4,128)S(1)} custom-call(f32[1056,384]{1,0:T(8,128)} %x_hbm.1), custom_call_target="tpu_custom_call" | custom-call | tf_op jit(solution)/shard_map/pallas_call | solution.py:817
  62.0 1.4 %copy.3 = f32[4,132,1056]{2,0,1:T(4,128)} copy(f32[4,132,1056]{2,0,1:T(4,128)S(1)} %bitcast.1) | data formatting | bytes 4460544

commit v6 on v5

--- a/solution.py
+++ b/solution.py
@@ -368,14 +368,8 @@
     barrier = pltpu.get_barrier_semaphore()
     for d in range(1, B):
         pl.semaphore_signal(barrier, inc=1, device_id=(l, lax.rem(b + d, B)), device_id_type=MESH)
-    facing = [jnp.where(inner, 3 * side, 1 + side) for side in range(2)]
-    for d in range(1, L):
-        other = lax.rem(l + d, L)
-        pl.semaphore_signal(barrier, inc=1, device_id=(other, b), device_id_type=MESH)
-        for side in range(2):
-            for core in range(2):
-                pl.semaphore_signal(barrier, inc=1, device_id=(other, facing[side] * 2 + core),
-                                    device_id_type=MESH)
+    for line in (lx, ly):
+        pl.semaphore_signal(barrier, inc=1, device_id=(line, b), device_id_type=MESH)
 
     def load(i):
         rows = pl.ds(pl.multiple_of(i * tile, tile), tile)
@@ -403,7 +397,7 @@
                            preferred_element_type=jnp.float32)
     stats[b] = line[:2]
 
-    pl.semaphore_wait(barrier, B - 1 + 5 * (L - 1))
+    pl.semaphore_wait(barrier, B - 1 + 2)
 
     def stat_copy(source, peer):
         return pltpu.make_async_remote_copy(
@@ -506,19 +500,21 @@
 
     first = align(jnp.minimum(b * share // 16 * 16, jnp.where(q == 0, size[D], R) - W))
 
+    def extract_one(k):
+        window = zbuf[k, pl.ds(first, W), :]
+        row = lax.broadcasted_iota(jnp.int32, (SP, W), 0)
+        hot = lax.broadcasted_iota(jnp.int32, (SP, W), 1) == row + (b * share - first)
+        hot = jnp.where(hot & (row < share), 1.0, 0.0).astype(jnp.bfloat16)
+        rows = lax.dot_general(hot, window, (((1,), (0,)), ((), ())),
+                               preferred_element_type=jnp.float32)
+        shr[k, l] = rows.astype(jnp.bfloat16)
+        share_copy(k, l, lx, 0).start()
+        share_copy(k, l, ly, 1).start()
+
     def extract(place):
         @pl.loop(0, 2)
         def _(core):
-            k = place * 2 + core
-            window = zbuf[k, pl.ds(first, W), :]
-            row = lax.broadcasted_iota(jnp.int32, (SP, W), 0)
-            hot = lax.broadcasted_iota(jnp.int32, (SP, W), 1) == row + (b * share - first)
-            hot = jnp.where(hot & (row < share), 1.0, 0.0).astype(jnp.bfloat16)
-            rows = lax.dot_general(hot, window, (((1,), (0,)), ((), ())),
-                                   preferred_element_type=jnp.float32)
-            shr[k, l] = rows.astype(jnp.bfloat16)
-            share_copy(k, l, lx, 0).start()
-            share_copy(k, l, ly, 1).start()
+            extract_one(place * 2 + core)
 
     def pass_on(place):
         @pl.loop(0, 2)
@@ -640,9 +636,10 @@
         for p in (N, C, F, M):
             z_copy(b, p, own_in, in_nbr).start()
     mate_own(b).start()
+    extract_one(b)
     make_hot()
     mate_own(mate).wait_recv()
-    extract(q)
+    extract_one(mate)
 
     @pl.when(inner)
     def _():
@@ -659,6 +656,9 @@
         extract(H[3])
         mate_take(1, (D, N, C))
         extract(H[1])
+        take(1, F, send_out)
+        take(3, F, send_in)
+        send_in(own(3), C).start()
 
     @pl.when(outer)
     def _():
@@ -669,6 +669,10 @@
         pass_on(q)
         take(2, F)
         take(2, C)
+        take(1, D)
+        mate_take(1, (D,))
+        extract(H[1])
+        pass_on(H[2])
         mate_take(2, (F, C))
     wait_diag(q)
     acc_lo[...] = product(q, 0, WS)
@@ -679,68 +683,56 @@
 
     @pl.when(inner)
     def _():
-        take(1, F, send_out)
-        take(3, F, send_in)
-        send_in(own(3), C).start()
         pass_on(H[3])
         take(3, M, send_in)
         send_in(own(3), D).start()
         take(0, D, send_out)
         take(0, C, send_out)
+        z_copy(b, N, own_in, in_nbr).start()
         pass_on(H[1])
         take(0, N)
         mate_take(3, (F, M))
         mate_take(0, (D, C, N))
         extract(H[0])
+        mate_take(1, (F,))
 
     @pl.when(outer)
     def _():
-        pass_on(H[2])
-        take(1, D)
-        mate_take(1, (D,))
-        extract(H[1])
         take(1, C)
-    wait_diag(second)
-    add_sides(second)
-    add_middle(second)
-
-    @pl.when(inner)
-    def _():
-        take(0, F, send_out)
-        z_copy(b, N, own_in, in_nbr).start()
-        mate_take(1, (F,))
-        mate_take(0, (F,))
-
-    @pl.when(outer)
-    def _():
         take(1, F)
-        pass_on(H[1])
         take(0, D)
         mate_take(0, (D,))
         extract(H[0])
+        pass_on(H[1])
         take(0, C)
         mate_take(1, (C, F))
+    wait_diag(second)
+    add_sides(second)
     wait_diag(third)
     add_sides(third)
 
-    pass_on(H[0])
-
-    @pl.when(inner)
-    def _():
+    @pl.when(inner)
+    def _():
+        take(0, F, send_out)
+        mate_take(0, (F,))
         finish_tiles(l)
         start_tiles(l)
-
+    pass_on(H[0])
+
+    @pl.when(inner)
+    def _():
         @pl.loop(0, 2)
         def _(n):
             j = jnp.where(n == 0, lx, ly)
             finish_tiles(j)
             start_tiles(j)
         send_in(own(3), N).start()
-        take(1, M)
         wait_diag(H[0])
         finish_tiles(ld)
         start_tiles(ld)
+        take(1, M)
         mate_take(1, (M,))
+    add_middle(second)
     add_middle(third)
 
     @pl.when(inner)

time: 63.6 us -> 62.9 us (0.989)
  Pallas kernels: 62 us -> 61.3 us
    pallas_call x1, Pallas kernels: 62 us -> 61.3 us  [line_call(): pl.pallas_call(functools.partial(line_kernel, L, B), out_shape=jax.ShapeD...]
where the time goes in v6:
time: 62.9 us; the launch traced here: 62.7 us
  Pallas kernels  61.3 us (97%)
  local copies, waits for them, and re-layouts  1.43 us (2%)
    pallas_call x1, Pallas kernels, line_call(): pl.pallas_call(functools.partial(line_kernel, L, B), out_shape=jax.ShapeD...  61.3 us
    unnamed x1, local copies, waits for them, and re-layouts  1.43 us

profile of v6, /device:TPU:0, one launch (start us, length us, event | category | flops | bytes accessed | tf_op | source)
XLA Modules:
  0.0 62.7 jit_solution(13382050671799321622)
XLA Ops:
  0.0 61.3 %shard_map.17 = f32[132,4,1056]{2,1,0:T(4,128)S(1)} custom-call(f32[1056,384]{1,0:T(8,128)} %x_hbm.1), custom_call_target="tpu_custom_call" | custom-call | tf_op jit(solution)/shard_map/pallas_call | solution.py:809
  61.3 1.4 %copy.3 = f32[4,132,1056]{2,0,1:T(4,128)} copy(f32[4,132,1056]{2,0,1:T(4,128)S(1)} %bitcast.1) | data formatting | bytes 4460544

commit v7 on v6

--- a/solution.py
+++ b/solution.py
@@ -485,14 +485,16 @@
             device_id=(l, mate), device_id_type=MESH)
 
     def share_copy(k, block, peer, way):
-        return pltpu.make_async_remote_copy(
-            src_ref=shr.at[k, block], dst_ref=shr.at[k, block], send_sem=shr_send,
+        part = shr.at[k, block, pl.ds(0, SR), :]
+        return pltpu.make_async_remote_copy(
+            src_ref=part, dst_ref=part, send_sem=shr_send,
             recv_sem=shr_recv.at[k, way], device_id=(peer, b), device_id_type=MESH)
 
-    cut = up_to(SP // 2, 16)
+    SR = up_to(share, 8)
+    cut = up_to(share // 2, 16)
 
     def diag_copy(k, block, peer, way):
-        rows = pl.ds(0, cut) if way == 0 else pl.ds(cut, SP - cut)
+        rows = pl.ds(0, cut) if way == 0 else pl.ds(cut, SR - cut)
         part = shr.at[k, block, rows, :]
         return pltpu.make_async_remote_copy(
             src_ref=part, dst_ref=part, send_sem=diag_send,
@@ -526,7 +528,7 @@
             diag_copy(k, ly, lx, 1).start()
 
     def wait_diag(place):
-        part = shr.at[pl.ds(place * 2, 2), ld]
+        part = shr.at[pl.ds(place * 2, 2), ld, pl.ds(0, SR), :]
         pltpu.make_async_remote_copy(
             src_ref=part, dst_ref=part, send_sem=diag_send, recv_sem=diag_recv.at[place],
             device_id=(l, b), device_id_type=MESH).wait_recv()
@@ -568,14 +570,14 @@
 
     def tile_copy(side, j, core, block, slot):
         return pltpu.make_async_remote_copy(
-            src_ref=tile_send.at[side, j, pl.ds(core * SP, SP), :],
-            dst_ref=tile_recv.at[block, :, pl.ds(pl.multiple_of(slot * 128, 128), 128)],
+            src_ref=tile_send.at[side, j, core, pl.ds(0, SR), :],
+            dst_ref=tile_recv.at[block, pl.ds(0, SR), pl.ds(pl.multiple_of(slot * 128, 128), 128)],
             send_sem=t_send, recv_sem=t_recv.at[block],
             device_id=(j, 6 * side + core), device_id_type=MESH)
 
     def make_hot():
-        shift = (lax.broadcasted_iota(jnp.int32, (SP, 128), 0)
-                 == lax.broadcasted_iota(jnp.int32, (SP, 128), 1) + jnp.where(c == 0, pad, 0))
+        shift = (lax.broadcasted_iota(jnp.int32, (SR, 128), 0)
+                 == lax.broadcasted_iota(jnp.int32, (SR, 128), 1) + jnp.where(c == 0, pad, 0))
         shift_ref[...] = jnp.where(shift, 1.0, 0.0).astype(jnp.bfloat16)
         row = lax.broadcasted_iota(jnp.int32, (512, WM), 0)
         lane = jnp.where(row < 256, row + half + pad, row - 256 + R // 2 + pad) - mid_lane
@@ -591,11 +593,11 @@
                 value = value + lax.dot_general(shr[k, j], zbuf[k, begin:begin + WS, :], NT,
                                                 preferred_element_type=jnp.float32)
             acc[rows, :] = value
-            turned = lax.dot_general((value / total).astype(jnp.bfloat16), shift_ref[...], TN,
+            turned = lax.dot_general((value[:SR] / total).astype(jnp.bfloat16), shift_ref[...], TN,
                                      preferred_element_type=jnp.float32)
             for core in range(2):
                 at = (WS - half if side else 0) + core * share
-                tile_send[side, j, core * SP:core * SP + share, :] = turned[at:at + share].astype(jnp.bfloat16)
+                tile_send[side, j, core, :share, :] = turned[at:at + share].astype(jnp.bfloat16)
 
     def start_tiles(j):
         for side in range(2):
@@ -603,7 +605,7 @@
                 tile_copy(side, j, core, l, b - 2).start()
 
     def wait_tile(block):
-        part = tile_recv.at[block]
+        part = tile_recv.at[block, pl.ds(0, SR), :]
         pltpu.make_async_remote_copy(
             src_ref=part, dst_ref=part, send_sem=t_send, recv_sem=t_recv.at[block],
             device_id=(l, b), device_id_type=MESH).wait_recv()
@@ -700,23 +702,29 @@
     def _():
         take(1, C)
         take(1, F)
+        pass_on(H[1])
+        mate_take(1, (C, F))
+    wait_diag(second)
+    add_sides(second)
+
+    @pl.when(inner)
+    def _():
+        take(0, F, send_out)
+    wait_diag(third)
+    add_sides(third)
+
+    @pl.when(inner)
+    def _():
+        mate_take(0, (F,))
+        finish_tiles(l)
+        start_tiles(l)
+
+    @pl.when(outer)
+    def _():
         take(0, D)
         mate_take(0, (D,))
         extract(H[0])
-        pass_on(H[1])
         take(0, C)
-        mate_take(1, (C, F))
-    wait_diag(second)
-    add_sides(second)
-    wait_diag(third)
-    add_sides(third)
-
-    @pl.when(inner)
-    def _():
-        take(0, F, send_out)
-        mate_take(0, (F,))
-        finish_tiles(l)
-        start_tiles(l)
     pass_on(H[0])
 
     @pl.when(inner)
@@ -782,7 +790,7 @@
         sent(zbuf.at[pl.ds(0, 2), pl.ds(0, far), :], out_send)
         sent(zbuf.at[0], in_send)
         sent(zbuf.at[pl.ds(0, 3)], mate_send)
-        sent(tile_send, t_send)
+        sent(tile_send.at[:, :, :, pl.ds(0, SR), :], t_send)
 
     @pl.when(outer)
     def _():
@@ -791,8 +799,8 @@
         sent(zbuf.at[pl.ds(0, 3), pl.ds(0, far), :], mate_send)
 
     sent(zbuf.at[0, pl.ds(0, R - size[D]), :], own_in)
-    sent(shr.at[pl.ds(0, L)], shr_send)
-    sent(shr.at[pl.ds(0, B // L)], diag_send)
+    sent(shr.at[pl.ds(0, L), :, pl.ds(0, SR), :], shr_send)
+    sent(shr.at[pl.ds(0, B // L), :, pl.ds(0, SR), :], diag_send)
 
 
 def line_call(L, B, series):
@@ -817,9 +825,9 @@
             pltpu.VMEM((L * SP, WS), jnp.float32),
             pltpu.VMEM((L * SP, WS), jnp.float32),
             pltpu.VMEM((L * SP, WM), jnp.float32),
-            pltpu.VMEM((2, L, 2 * SP, 128), jnp.bfloat16),
+            pltpu.VMEM((2, L, 2, SP, 128), jnp.bfloat16),
             pltpu.VMEM((L, SP, 512), jnp.bfloat16),
-            pltpu.VMEM((SP, 128), jnp.bfloat16),
+            pltpu.VMEM((up_to(share, 8), 128), jnp.bfloat16),
             pltpu.VMEM((512, WM), jnp.bfloat16),
             pltpu.VMEM((R, 128), jnp.float32),
             pltpu.VMEM((B, 2, R), jnp.float32),

time: 62.9 us -> 61.2 us (0.973)
  Pallas kernels: 61.3 us -> 59.7 us
    pallas_call x1, Pallas kernels: 61.3 us -> 59.7 us  [line_call(): pl.pallas_call(functools.partial(line_kernel, L, B), out_shape=jax.ShapeD...]
where the time goes in v7:
time: 61.2 us; the launch traced here: 61.1 us
  Pallas kernels  59.7 us (98%)
  local copies, waits for them, and re-layouts  1.43 us (2%)
    pallas_call x1, Pallas kernels, line_call(): pl.pallas_call(functools.partial(line_kernel, L, B), out_shape=jax.ShapeD...  59.7 us
    unnamed x1, local copies, waits for them, and re-layouts  1.43 us

profile of v7, /device:TPU:0, one launch (start us, length us, event | category | flops | bytes accessed | tf_op | source)
XLA Modules:
  0.0 61.1 jit_solution(7883981474412455768)
XLA Ops:
  0.0 59.7 %shard_map.17 = f32[132,4,1056]{2,1,0:T(4,128)S(1)} custom-call(f32[1056,384]{1,0:T(8,128)} %x_hbm.1), custom_call_target="tpu_custom_call" | custom-call | tf_op jit(solution)/shard_map/pallas_call | solution.py:817
  59.7 1.4 %copy.3 = f32[4,132,1056]{2,0,1:T(4,128)} copy(f32[4,132,1056]{2,0,1:T(4,128)S(1)} %bitcast.1) | data formatting | bytes 4460544

commit v8 on v7

--- a/solution.py
+++ b/solution.py
@@ -326,7 +326,7 @@
             share_copy(k, l, other).wait_send()
 
 
-F, M, C, N, D = range(5)
+F, M2, M1, C, N1, N2, D = range(7)
 
 
 def line_kernel(L, B, x_hbm, o_ref, zbuf, shr, acc_lo, acc_hi, acc_mid, tile_send, tile_recv, shift_ref, place_ref,
@@ -341,9 +341,11 @@
     pad = share - 128
     W = min(up_to(share + 15, 16), R)
     low, high = R - (3 * half - pad) // 16 * 16, (3 * half - pad) // 16 * 16
-    edges = [0, low, (R // 2 - pad) // 16 * 16, up_to(R // 2 + pad, 16), high, R]
-    size = [edges[p + 1] - edges[p] for p in range(5)]
-    far = size[F] + size[C] + size[D]
+    split = (3 * half - share) // 16 * 16
+    edges = [0, low, R - split, (R // 2 - pad) // 16 * 16]
+    edges = edges + [R - x for x in reversed(edges)]
+    size = [edges[p + 1] - edges[p] for p in range(7)]
+    far = R - size[M2] - size[M1] - size[N1]
     tile = largest_tile(R, 352)
     RAW = raw.shape[1]
     WS = acc_lo.shape[1]
@@ -363,7 +365,7 @@
     def align(value, unit=16):
         return pl.multiple_of(value, unit)
 
-    start = [align(jnp.where(upper, edges[p], edges[4 - p])) for p in range(5)]
+    start = [align(jnp.where(upper, edges[p], edges[6 - p])) for p in range(7)]
 
     barrier = pltpu.get_barrier_semaphore()
     for d in range(1, B):
@@ -458,7 +460,7 @@
         part = zbuf.at[k, pl.ds(align(start[p] + skip), size[p] - skip), :]
         return pltpu.make_async_remote_copy(
             src_ref=part, dst_ref=part, send_sem=send_sem,
-            recv_sem=z_recv.at[k, jnp.where(upper, p, 4 - p)], device_id=(l, peer), device_id_type=MESH)
+            recv_sem=z_recv.at[k, jnp.where(upper, p, 6 - p)], device_id=(l, peer), device_id_type=MESH)
 
     def first_copy(k, p, peer):
         return z_copy(k, p, first_send, peer, RAW)
@@ -583,6 +585,10 @@
         lane = jnp.where(row < 256, row + half + pad, row - 256 + R // 2 + pad) - mid_lane
         hot = lax.broadcasted_iota(jnp.int32, (512, WM), 1) == lane
         place_ref[...] = jnp.where(hot, 1.0, 0.0).astype(jnp.bfloat16)
+        for side, slot in ((0, 0), (3, 3)):
+            @pl.when(q == side)
+            def _():
+                tile_recv[:, :, slot * 128:slot * 128 + 128] = jnp.zeros((L, SP, 128), jnp.bfloat16)
 
     def finish_tiles(j):
         rows = pl.ds(pl.multiple_of(j * SP, SP), SP)
@@ -599,13 +605,18 @@
                 at = (WS - half if side else 0) + core * share
                 tile_send[side, j, core, :share, :] = turned[at:at + share].astype(jnp.bfloat16)
 
+    def tile_copies(j, act):
+        for side, skipped in ((0, 2), (1, 5)):
+            @pl.when(b != skipped)
+            def _():
+                for core in range(2):
+                    act(tile_copy(side, j, core, l, b - 2))
+
     def start_tiles(j):
-        for side in range(2):
-            for core in range(2):
-                tile_copy(side, j, core, l, b - 2).start()
+        tile_copies(j, lambda copy: copy.start())
 
     def wait_tile(block):
-        part = tile_recv.at[block, pl.ds(0, SR), :]
+        part = tile_recv.at[block, pl.ds(0, SR), pl.ds(0, 384)]
         pltpu.make_async_remote_copy(
             src_ref=part, dst_ref=part, send_sem=t_send, recv_sem=t_recv.at[block],
             device_id=(l, b), device_id_type=MESH).wait_recv()
@@ -628,14 +639,14 @@
 
     @pl.when(inner)
     def _():
-        for p in (M, C, D):
+        for p in (M2, M1, C, D):
             z_copy(b, p, own_in, in_nbr).start()
-        for p in (F, C):
+        for p in (F, C, N2):
             z_copy(b, p, own_out, out_nbr).start()
 
     @pl.when(outer)
     def _():
-        for p in (N, C, F, M):
+        for p in (N2, N1, C, F, M1, M2):
             z_copy(b, p, own_in, in_nbr).start()
     mate_own(b).start()
     extract_one(b)
@@ -650,13 +661,15 @@
         take(1, D, send_out, True)
         take(3, D, None, True)
         pass_on(q)
-        take(1, N)
-        take(3, N)
+        take(1, N2, send_out)
+        take(3, N2)
+        take(1, N1)
+        take(3, N1)
         take(1, C, send_out)
         take(3, C)
-        mate_take(3, (D, N, C))
+        mate_take(3, (D, N2, N1, C))
         extract(H[3])
-        mate_take(1, (D, N, C))
+        mate_take(1, (D, N2, N1, C))
         extract(H[1])
         take(1, F, send_out)
         take(3, F, send_in)
@@ -671,11 +684,12 @@
         pass_on(q)
         take(2, F)
         take(2, C)
+        take(2, N2)
+        pass_on(H[2])
         take(1, D)
         mate_take(1, (D,))
         extract(H[1])
-        pass_on(H[2])
-        mate_take(2, (F, C))
+        mate_take(2, (F, C, N2))
     wait_diag(q)
     acc_lo[...] = product(q, 0, WS)
     acc_hi[...] = product(q, hi_lane, WS)
@@ -686,30 +700,40 @@
     @pl.when(inner)
     def _():
         pass_on(H[3])
-        take(3, M, send_in)
+        take(3, M1, send_in)
+        take(3, M2, send_in)
         send_in(own(3), D).start()
         take(0, D, send_out)
         take(0, C, send_out)
-        z_copy(b, N, own_in, in_nbr).start()
+        for p in (N1, N2):
+            z_copy(b, p, own_in, in_nbr).start()
         pass_on(H[1])
-        take(0, N)
-        mate_take(3, (F, M))
-        mate_take(0, (D, C, N))
+        take(0, N1)
+        take(0, N2, send_out)
+        mate_take(3, (F, M1, M2))
+        mate_take(0, (D, C, N1, N2))
         extract(H[0])
         mate_take(1, (F,))
 
     @pl.when(outer)
     def _():
+        take(1, N2)
         take(1, C)
         take(1, F)
         pass_on(H[1])
-        mate_take(1, (C, F))
+        mate_take(1, (N2, C, F))
     wait_diag(second)
     add_sides(second)
 
     @pl.when(inner)
     def _():
         take(0, F, send_out)
+
+    @pl.when(outer)
+    def _():
+        take(0, D)
+        mate_take(0, (D,))
+        extract(H[0])
     wait_diag(third)
     add_sides(third)
 
@@ -721,10 +745,8 @@
 
     @pl.when(outer)
     def _():
-        take(0, D)
-        mate_take(0, (D,))
-        extract(H[0])
         take(0, C)
+        take(0, N2)
     pass_on(H[0])
 
     @pl.when(inner)
@@ -734,24 +756,27 @@
             j = jnp.where(n == 0, lx, ly)
             finish_tiles(j)
             start_tiles(j)
-        send_in(own(3), N).start()
+        for p in (N1, N2):
+            send_in(own(3), p).start()
         wait_diag(H[0])
         finish_tiles(ld)
         start_tiles(ld)
-        take(1, M)
-        mate_take(1, (M,))
+        for p in (M1, M2):
+            take(1, p)
+        mate_take(1, (M1, M2))
     add_middle(second)
     add_middle(third)
 
     @pl.when(inner)
     def _():
-        take(0, M)
-        mate_take(0, (M,))
+        for p in (M1, M2):
+            take(0, p)
+        mate_take(0, (M1, M2))
 
     @pl.when(outer)
     def _():
         take(0, F)
-        mate_take(0, (C, F))
+        mate_take(0, (C, N2, F))
         wait_diag(H[0])
         add_sides(H[0])
     add_middle(H[0])
@@ -765,8 +790,10 @@
     @pl.when(outer)
     def _():
         place = lax.broadcasted_iota(jnp.int32, (share, WM), 1) + mid_lane
-        inside = ((place >= half + pad) & (place < half + pad + 256)
-                  | (place >= R // 2 + pad) & (place < R // 2 + pad + 256))
+        first_lane = half + pad + jnp.where(upper, 0, 128)
+        last_lane = R // 2 + pad + jnp.where(upper, 128, 256)
+        inside = ((place >= first_lane) & (place < half + pad + 256)
+                  | (place >= R // 2 + pad) & (place < last_lane))
         for d in (l, lx, ly, ld):
             wait_tile(d)
             placed = lax.dot_general(tile_recv[d], place_ref[...], (((1,), (0,)), ((), ())),
@@ -784,13 +811,17 @@
 
     @pl.when(inner)
     def _():
-        sent(zbuf.at[0, pl.ds(0, size[F] + size[C]), :], own_out)
+        sent(zbuf.at[0, pl.ds(0, size[F] + size[C] + size[N2]), :], own_out)
         sent(zbuf.at[pl.ds(0, 2), pl.ds(0, size[D] - RAW), :], first_send)
         sent(raw, raw_send)
         sent(zbuf.at[pl.ds(0, 2), pl.ds(0, far), :], out_send)
         sent(zbuf.at[0], in_send)
         sent(zbuf.at[pl.ds(0, 3)], mate_send)
-        sent(tile_send.at[:, :, :, pl.ds(0, SR), :], t_send)
+        for skipped in (True, False):
+            @pl.when(((b == 2) | (b == 5)) == skipped)
+            def _():
+                sides = 1 if skipped else 2
+                sent(tile_send.at[pl.ds(0, sides), :, :, pl.ds(0, SR), :], t_send)
 
     @pl.when(outer)
     def _():
@@ -833,7 +864,7 @@
             pltpu.VMEM((B, 2, R), jnp.float32),
             pltpu.VMEM((R, T), jnp.float32),
             pltpu.VMEM((2, (R - high) // 32 * 16, T), jnp.float32),
-            dma((B, 5)), dma, dma, dma, dma, dma, dma, dma, dma((2,)), dma,
+            dma((B, 7)), dma, dma, dma, dma, dma, dma, dma, dma((2,)), dma,
             dma((B, 2)), dma, dma((B // 2,)), dma, dma((L,)), dma,
             dma, dma, dma((R // largest_tile(R, 352),)),
         ],

time: 61.2 us -> 59.3 us (0.969)
  Pallas kernels: 59.7 us -> 57.8 us
    pallas_call x1, Pallas kernels: 59.7 us -> 57.8 us  [line_call(): pl.pallas_call(functools.partial(line_kernel, L, B), out_shape=jax.ShapeD...]
where the time goes in v8:
time: 59.3 us; the launch traced here: 59.2 us
  Pallas kernels  57.8 us (97%)
  local copies, waits for them, and re-layouts  1.43 us (2%)
    pallas_call x1, Pallas kernels, line_call(): pl.pallas_call(functools.partial(line_kernel, L, B), out_shape=jax.ShapeD...  57.8 us
    unnamed x1, local copies, waits for them, and re-layouts  1.43 us

profile of v8, /device:TPU:0, one launch (start us, length us, event | category | flops | bytes accessed | tf_op | source)
XLA Modules:
  0.0 59.2 jit_solution(395580624648725836)
XLA Ops:
  0.0 57.8 %shard_map.17 = f32[132,4,1056]{2,1,0:T(4,128)S(1)} custom-call(f32[1056,384]{1,0:T(8,128)} %x_hbm.1), custom_call_target="tpu_custom_call" | custom-call | tf_op jit(solution)/shard_map/pallas_call | solution.py:848
  57.8 1.4 %copy.3 = f32[4,132,1056]{2,0,1:T(4,128)} copy(f32[4,132,1056]{2,0,1:T(4,128)S(1)} %bitcast.1) | data formatting | bytes 4460544

commit v9 on v8

--- a/solution.py
+++ b/solution.py
@@ -421,7 +421,7 @@
 
     @pl.when(outer)
     def _():
-        raw_copy(D, 1, in_nbr).start()
+        raw_copy(F, 1, in_nbr).start()
 
     gathered = stats.at[pl.ds(0, B - 1)]
     all_stats = pltpu.make_async_remote_copy(
@@ -465,9 +465,9 @@
     def first_copy(k, p, peer):
         return z_copy(k, p, first_send, peer, RAW)
 
-    def unpack(slot, k):
-        raw_copy(D, slot, b).wait_recv()
-        rows = pl.ds(start[D], RAW)
+    def unpack(slot, k, p):
+        raw_copy(p, slot, b).wait_recv()
+        rows = pl.ds(start[p], RAW)
         z = (raw[slot] - cols[rows, 0:1]) * cols[rows, 1:2]
         zbuf[k, rows, :] = z.astype(jnp.bfloat16)
 
@@ -594,8 +594,7 @@
         rows = pl.ds(pl.multiple_of(j * SP, SP), SP)
         for side, acc, begin in ((0, acc_lo, 0), (1, acc_hi, hi_lane)):
             value = acc[rows, :]
-            for core in range(2):
-                k = H[0] * 2 + core
+            for k in (H[3] * 2, H[3] * 2 + 1, H[0] * 2, H[0] * 2 + 1):
                 value = value + lax.dot_general(shr[k, j], zbuf[k, begin:begin + WS, :], NT,
                                                 preferred_element_type=jnp.float32)
             acc[rows, :] = value
@@ -627,26 +626,21 @@
     def _():
         first_copy(b, D, out_nbr).start()
 
-    @pl.when(outer)
-    def _():
-        first_copy(b, D, in_nbr).start()
     normalise(start[F], size[F])
 
+    first_copy(b, F, in_nbr).start()
+    normalise(low, high - low)
+
     @pl.when(inner)
     def _():
-        first_copy(b, F, in_nbr).start()
-    normalise(low, high - low)
-
-    @pl.when(inner)
-    def _():
-        for p in (M2, M1, C, D):
+        for p in (M2, M1, C):
             z_copy(b, p, own_in, in_nbr).start()
         for p in (F, C, N2):
             z_copy(b, p, own_out, out_nbr).start()
 
     @pl.when(outer)
     def _():
-        for p in (N2, N1, C, F, M1, M2):
+        for p in (M2, M1, C, D, N2, N1):
             z_copy(b, p, own_in, in_nbr).start()
     mate_own(b).start()
     extract_one(b)
@@ -656,28 +650,26 @@
 
     @pl.when(inner)
     def _():
-        unpack(0, own(1))
-        unpack(1, own(3))
+        unpack(0, own(1), D)
+        unpack(1, own(3), F)
         take(1, D, send_out, True)
-        take(3, D, None, True)
+        take(3, F, send_in, True)
         pass_on(q)
         take(1, N2, send_out)
-        take(3, N2)
+        take(3, M2, send_in)
         take(1, N1)
-        take(3, N1)
+        take(3, M1, send_in)
         take(1, C, send_out)
-        take(3, C)
-        mate_take(3, (D, N2, N1, C))
-        extract(H[3])
+        take(3, C, send_in)
+        z_copy(b, D, own_in, in_nbr).start()
         mate_take(1, (D, N2, N1, C))
         extract(H[1])
-        take(1, F, send_out)
-        take(3, F, send_in)
-        send_in(own(3), C).start()
+        take(0, D, send_out)
+        take(3, D, send_in)
 
     @pl.when(outer)
     def _():
-        unpack(0, own(2))
+        unpack(0, own(2), D)
         take(2, D, None, True)
         mate_take(2, (D,))
         extract(H[2])
@@ -695,62 +687,55 @@
     acc_hi[...] = product(q, hi_lane, WS)
     acc_mid[...] = product(q, mid_lane, WM)
 
-    second, third = jnp.where(inner, H[3], H[2]), H[1]
+    second, third = jnp.where(inner, H[1], H[2]), jnp.where(inner, H[3], H[1])
 
     @pl.when(inner)
     def _():
-        pass_on(H[3])
-        take(3, M1, send_in)
-        take(3, M2, send_in)
-        send_in(own(3), D).start()
-        take(0, D, send_out)
+        pass_on(H[1])
+        take(0, N2, send_out)
+        take(0, N1)
         take(0, C, send_out)
-        for p in (N1, N2):
-            z_copy(b, p, own_in, in_nbr).start()
-        pass_on(H[1])
-        take(0, N1)
-        take(0, N2, send_out)
-        mate_take(3, (F, M1, M2))
-        mate_take(0, (D, C, N1, N2))
+        mate_take(0, (D, N2, N1, C))
         extract(H[0])
+        take(3, N2)
+        take(3, N1)
+        mate_take(3, (C, D, N2, N1))
+        extract(H[3])
+        take(1, F, send_out)
         mate_take(1, (F,))
 
     @pl.when(outer)
     def _():
         take(1, N2)
         take(1, C)
-        take(1, F)
         pass_on(H[1])
-        mate_take(1, (N2, C, F))
     wait_diag(second)
     add_sides(second)
-
-    @pl.when(inner)
-    def _():
-        take(0, F, send_out)
 
     @pl.when(outer)
     def _():
         take(0, D)
         mate_take(0, (D,))
         extract(H[0])
-    wait_diag(third)
-    add_sides(third)
+        take(0, N2)
+        take(0, C)
+        take(1, F)
+        mate_take(1, (N2, C, F))
+        wait_diag(H[1])
+        add_sides(H[1])
+    pass_on(H[0])
 
     @pl.when(inner)
     def _():
+        take(0, F, send_out)
+        for p in (N1, N2):
+            z_copy(b, p, own_in, in_nbr).start()
+        mate_take(3, (F, M1, M2))
         mate_take(0, (F,))
         finish_tiles(l)
         start_tiles(l)
-
-    @pl.when(outer)
-    def _():
-        take(0, C)
-        take(0, N2)
-    pass_on(H[0])
-
-    @pl.when(inner)
-    def _():
+        pass_on(H[3])
+
         @pl.loop(0, 2)
         def _(n):
             j = jnp.where(n == 0, lx, ly)
@@ -759,6 +744,7 @@
         for p in (N1, N2):
             send_in(own(3), p).start()
         wait_diag(H[0])
+        wait_diag(H[3])
         finish_tiles(ld)
         start_tiles(ld)
         for p in (M1, M2):

time: 59.3 us -> 57.7 us (0.973)
  Pallas kernels: 57.8 us -> 56 us
    pallas_call x1, Pallas kernels: 57.8 us -> 56 us  [line_call(): pl.pallas_call(functools.partial(line_kernel, L, B), out_shape=jax.ShapeD...]
where the time goes in v9:
time: 57.7 us; the launch traced here: 57.5 us
  Pallas kernels  56 us (97%)
  local copies, waits for them, and re-layouts  1.43 us (2%)
    pallas_call x1, Pallas kernels, line_call(): pl.pallas_call(functools.partial(line_kernel, L, B), out_shape=jax.ShapeD...  56 us
    unnamed x1, local copies, waits for them, and re-layouts  1.43 us

profile of v9, /device:TPU:0, one launch (start us, length us, event | category | flops | bytes accessed | tf_op | source)
XLA Modules:
  0.0 57.5 jit_solution(7505492383820518483)
XLA Ops:
  0.0 56.0 %shard_map.17 = f32[132,4,1056]{2,1,0:T(4,128)S(1)} custom-call(f32[1056,384]{1,0:T(8,128)} %x_hbm.1), custom_call_target="tpu_custom_call" | custom-call | tf_op jit(solution)/shard_map/pallas_call | solution.py:834
  56.0 1.4 %copy.3 = f32[4,132,1056]{2,0,1:T(4,128)} copy(f32[4,132,1056]{2,0,1:T(4,128)S(1)} %bitcast.1) | data formatting | bytes 4460544

commit v10 on v9

--- a/solution.py
+++ b/solution.py
@@ -394,9 +394,20 @@
         cols[rows, :] = jnp.where(lane == 0, mean, jnp.where(lane == 1, m2, 0.0))
 
     pick = (lax.broadcasted_iota(jnp.int32, (8, 128), 0)
-            == lax.broadcasted_iota(jnp.int32, (8, 128), 1)).astype(jnp.float32)
-    line = lax.dot_general(pick, cols[...], NT, precision=lax.Precision.HIGHEST,
-                           preferred_element_type=jnp.float32)
+            == lax.broadcasted_iota(jnp.int32, (8, 128), 1)).astype(jnp.bfloat16)
+
+    def in_parts(x):
+        top = x.astype(jnp.bfloat16)
+        rest = x - top.astype(jnp.float32)
+        middle = rest.astype(jnp.bfloat16)
+        return top, middle, (rest - middle.astype(jnp.float32)).astype(jnp.bfloat16)
+
+    def exact_dot(parts, dot):
+        top, middle, low_part = [dot(part) for part in parts]
+        return top + middle + low_part
+
+    line = exact_dot(in_parts(cols[...]), lambda part: lax.dot_general(
+        pick, part, NT, preferred_element_type=jnp.float32))
     stats[b] = line[:2]
 
     pl.semaphore_wait(barrier, B - 1 + 2)
@@ -440,8 +451,8 @@
     scale = lax.rsqrt(square / total + epsilon)
     sub = lax.broadcasted_iota(jnp.int32, (8, R), 0)
     both = jnp.where(sub == 0, mean, jnp.where(sub == 1, scale, 0.0))
-    cols[...] = lax.dot_general(both, pick, TN, precision=lax.Precision.HIGHEST,
-                                preferred_element_type=jnp.float32)
+    cols[...] = exact_dot(in_parts(both), lambda part: lax.dot_general(
+        part, pick, TN, preferred_element_type=jnp.float32))
 
     def normalise(begin, count):
         unit = count if count <= 288 else largest_tile(count, 128)
@@ -590,15 +601,20 @@
             def _():
                 tile_recv[:, :, slot * 128:slot * 128 + 128] = jnp.zeros((L, SP, 128), jnp.bfloat16)
 
-    def finish_tiles(j):
+    def add_rows(j, place):
         rows = pl.ds(pl.multiple_of(j * SP, SP), SP)
-        for side, acc, begin in ((0, acc_lo, 0), (1, acc_hi, hi_lane)):
+        for acc, begin in ((acc_lo, 0), (acc_hi, hi_lane)):
             value = acc[rows, :]
-            for k in (H[3] * 2, H[3] * 2 + 1, H[0] * 2, H[0] * 2 + 1):
+            for core in range(2):
+                k = place * 2 + core
                 value = value + lax.dot_general(shr[k, j], zbuf[k, begin:begin + WS, :], NT,
                                                 preferred_element_type=jnp.float32)
             acc[rows, :] = value
-            turned = lax.dot_general((value[:SR] / total).astype(jnp.bfloat16), shift_ref[...], TN,
+
+    def turn_tiles(j):
+        rows = pl.ds(pl.multiple_of(j * SP, SP), SP)
+        for side, acc in ((0, acc_lo), (1, acc_hi)):
+            turned = lax.dot_general((acc[rows, :][:SR] / total).astype(jnp.bfloat16), shift_ref[...], TN,
                                      preferred_element_type=jnp.float32)
             for core in range(2):
                 at = (WS - half if side else 0) + core * share
@@ -732,20 +748,26 @@
             z_copy(b, p, own_in, in_nbr).start()
         mate_take(3, (F, M1, M2))
         mate_take(0, (F,))
-        finish_tiles(l)
+        add_rows(l, H[3])
+        add_rows(l, H[0])
+        turn_tiles(l)
         start_tiles(l)
         pass_on(H[3])
 
         @pl.loop(0, 2)
         def _(n):
             j = jnp.where(n == 0, lx, ly)
-            finish_tiles(j)
+            add_rows(j, H[3])
+            add_rows(j, H[0])
+            turn_tiles(j)
             start_tiles(j)
         for p in (N1, N2):
             send_in(own(3), p).start()
         wait_diag(H[0])
+        add_rows(ld, H[0])
         wait_diag(H[3])
-        finish_tiles(ld)
+        add_rows(ld, H[3])
+        turn_tiles(ld)
         start_tiles(ld)
         for p in (M1, M2):
             take(1, p)
@@ -753,28 +775,46 @@
     add_middle(second)
     add_middle(third)
 
+    def put(lanes, acc, begin=0):
+        for j in range(L):
+            part = acc[j * SP:j * SP + share, :][:, begin:begin + lanes.stop - lanes.start]
+            o_ref[:, j, lanes] = part / total
+
     @pl.when(inner)
     def _():
         for p in (M1, M2):
             take(0, p)
         mate_take(0, (M1, M2))
+        add_middle(H[0])
+        put(slice(0, mid_lane), acc_lo)
+        put(slice(mid_lane, mid_lane + WM), acc_mid)
+        put(slice(mid_lane + WM, R), acc_hi, mid_lane + WM - hi_lane)
+
+    lanes_lo = mid_lane, up_to(R // 2 + pad, 128)
+    lanes_hi = (R // 2 - pad) // 128 * 128, mid_lane + WM
 
     @pl.when(outer)
     def _():
+        mate_take(0, (N2, C))
+        wait_diag(H[0])
+        for end, acc, begin, (first_mid, last_mid) in ((0, acc_lo, 0, lanes_lo), (3, acc_hi, hi_lane, lanes_hi)):
+            @pl.when(q == end)
+            def _():
+                acc[...] += product(H[0], begin, WS)
+                inner_lanes = slice(first_mid - mid_lane, last_mid - mid_lane)
+                acc_mid[:, inner_lanes] += product(H[0], first_mid, last_mid - first_mid)
+                put(slice(first_mid, last_mid), acc_mid, first_mid - mid_lane)
+                if end:
+                    put(slice(last_mid, R), acc, last_mid - hi_lane)
+                else:
+                    put(slice(0, first_mid), acc)
         take(0, F)
-        mate_take(0, (C, N2, F))
-        wait_diag(H[0])
-        add_sides(H[0])
-    add_middle(H[0])
-
-    for j in range(L):
-        rows = slice(j * SP, j * SP + share)
-        o_ref[:, j, :mid_lane] = acc_lo[rows, :mid_lane] / total
-        o_ref[:, j, mid_lane:mid_lane + WM] = acc_mid[rows, :] / total
-        o_ref[:, j, mid_lane + WM:] = acc_hi[rows, :][:, mid_lane + WM - hi_lane:] / total
-
-    @pl.when(outer)
-    def _():
+        mate_take(0, (F,))
+        for end, acc, begin in ((3, acc_lo, 0), (0, acc_hi, hi_lane)):
+            @pl.when(q == end)
+            def _():
+                acc[...] += product(H[0], begin, WS)
+                put(slice(begin, begin + WS), acc)
         place = lax.broadcasted_iota(jnp.int32, (share, WM), 1) + mid_lane
         first_lane = half + pad + jnp.where(upper, 0, 128)
         last_lane = R // 2 + pad + jnp.where(upper, 128, 256)

time: 57.7 us -> 58 us (level)
  no operation moved by 1% of the time
where the time goes in v10:
time: 58 us; the launch traced here: 57.8 us
  Pallas kernels  56.4 us (97%)
  local copies, waits for them, and re-layouts  1.43 us (2%)
    pallas_call x1, Pallas kernels, line_call(): pl.pallas_call(functools.partial(line_kernel, L, B), out_shape=jax.ShapeD...  56.4 us
    unnamed x1, local copies, waits for them, and re-layouts  1.43 us

profile of v10, /device:TPU:0, one launch (start us, length us, event | category | flops | bytes accessed | tf_op | source)
XLA Modules:
  0.0 57.8 jit_solution(1205153671722085021)
XLA Ops:
  0.0 56.4 %shard_map.17 = f32[132,4,1056]{2,1,0:T(4,128)S(1)} custom-call(f32[1056,384]{1,0:T(8,128)} %x_hbm.1), custom_call_target="tpu_custom_call" | custom-call | tf_op jit(solution)/shard_map/pallas_call | solution.py:874
  56.4 1.4 %copy.3 = f32[4,132,1056]{2,0,1:T(4,128)} copy(f32[4,132,1056]{2,0,1:T(4,128)S(1)} %bitcast.1) | data formatting | bytes 4460544

commit v11 on v10

--- a/solution.py
+++ b/solution.py
@@ -345,7 +345,8 @@
     edges = [0, low, R - split, (R // 2 - pad) // 16 * 16]
     edges = edges + [R - x for x in reversed(edges)]
     size = [edges[p + 1] - edges[p] for p in range(7)]
-    far = R - size[M2] - size[M1] - size[N1]
+    narrow = size[C] // 2
+    far = R - size[M2] - size[M1] - size[N1] - narrow
     tile = largest_tile(R, 352)
     RAW = raw.shape[1]
     WS = acc_lo.shape[1]
@@ -366,6 +367,7 @@
         return pl.multiple_of(value, unit)
 
     start = [align(jnp.where(upper, edges[p], edges[6 - p])) for p in range(7)]
+    narrow_start = align(jnp.where(upper, R // 2 - narrow, R // 2))
 
     barrier = pltpu.get_barrier_semaphore()
     for d in range(1, B):
@@ -467,8 +469,11 @@
         else:
             pl.loop(0, count // unit)(chunk)
 
-    def z_copy(k, p, send_sem, peer, skip=0):
-        part = zbuf.at[k, pl.ds(align(start[p] + skip), size[p] - skip), :]
+    def z_copy(k, p, send_sem, peer, skip=0, to_end=False):
+        begin, rows = align(start[p] + skip), size[p] - skip
+        if to_end and p == C:
+            begin, rows = narrow_start, narrow
+        part = zbuf.at[k, pl.ds(begin, rows), :]
         return pltpu.make_async_remote_copy(
             src_ref=part, dst_ref=part, send_sem=send_sem,
             recv_sem=z_recv.at[k, jnp.where(upper, p, 6 - p)], device_id=(l, peer), device_id_type=MESH)
@@ -483,13 +488,13 @@
         zbuf[k, rows, :] = z.astype(jnp.bfloat16)
 
     def send_out(k, p):
-        return z_copy(k, p, out_send, out_nbr)
+        return z_copy(k, p, out_send, out_nbr, 0, True)
 
     def send_in(k, p):
         return z_copy(k, p, in_send, in_nbr)
 
-    def mate_copy(k, p):
-        return z_copy(k, p, mate_send, mate)
+    def mate_copy(k, p, to_end=False):
+        return z_copy(k, p, mate_send, mate, 0, to_end)
 
     def mate_own(k):
         part = zbuf.at[k]
@@ -568,18 +573,24 @@
     def other(h):
         return H[h] * 2 + (1 - c)
 
-    def take(h, p, onward=None, first=False):
+    def take(h, p, onward=None, first=False, to_end=False):
         if first:
             first_copy(own(h), p, mate).wait_recv()
         else:
-            mate_copy(own(h), p).wait_recv()
+            mate_copy(own(h), p, to_end).wait_recv()
         if onward is not None:
             onward(own(h), p).start()
-        mate_copy(own(h), p).start()
-
-    def mate_take(h, pieces):
+        mate_copy(own(h), p, to_end).start()
+
+    def mate_take(h, pieces, to_end=False):
         for p in pieces:
-            mate_copy(other(h), p).wait_recv()
+            mate_copy(other(h), p, to_end).wait_recv()
+
+    def take_end(h, p):
+        take(h, p, to_end=True)
+
+    def mate_take_end(h, pieces):
+        mate_take(h, pieces, True)
 
     def tile_copy(side, j, core, block, slot):
         return pltpu.make_async_remote_copy(
@@ -589,11 +600,14 @@
             device_id=(j, 6 * side + core), device_id_type=MESH)
 
     def make_hot():
-        shift = (lax.broadcasted_iota(jnp.int32, (SR, 128), 0)
-                 == lax.broadcasted_iota(jnp.int32, (SR, 128), 1) + jnp.where(c == 0, pad, 0))
-        shift_ref[...] = jnp.where(shift, 1.0, 0.0).astype(jnp.bfloat16)
+        for side, skip in ((0, jnp.where(b == 5, 0, pad)), (1, jnp.where(b == 2, pad, 0))):
+            shift = (lax.broadcasted_iota(jnp.int32, (SR, 128), 0)
+                     == lax.broadcasted_iota(jnp.int32, (SR, 128), 1) + skip)
+            shift_ref[side] = jnp.where(shift, 1.0, 0.0).astype(jnp.bfloat16)
         row = lax.broadcasted_iota(jnp.int32, (512, WM), 0)
-        lane = jnp.where(row < 256, row + half + pad, row - 256 + R // 2 + pad) - mid_lane
+        slot = row // 128
+        shifted = slot < jnp.where(upper, 1, 3)
+        lane = half - mid_lane + slot * (share - 128) + row + jnp.where(shifted, pad, 0)
         hot = lax.broadcasted_iota(jnp.int32, (512, WM), 1) == lane
         place_ref[...] = jnp.where(hot, 1.0, 0.0).astype(jnp.bfloat16)
         for side, slot in ((0, 0), (3, 3)):
@@ -614,7 +628,7 @@
     def turn_tiles(j):
         rows = pl.ds(pl.multiple_of(j * SP, SP), SP)
         for side, acc in ((0, acc_lo), (1, acc_hi)):
-            turned = lax.dot_general((acc[rows, :][:SR] / total).astype(jnp.bfloat16), shift_ref[...], TN,
+            turned = lax.dot_general((acc[rows, :][:SR] / total).astype(jnp.bfloat16), shift_ref[side], TN,
                                      preferred_element_type=jnp.float32)
             for core in range(2):
                 at = (WS - half if side else 0) + core * share
@@ -652,7 +666,7 @@
         for p in (M2, M1, C):
             z_copy(b, p, own_in, in_nbr).start()
         for p in (F, C, N2):
-            z_copy(b, p, own_out, out_nbr).start()
+            z_copy(b, p, own_out, out_nbr, 0, True).start()
 
     @pl.when(outer)
     def _():
@@ -690,14 +704,14 @@
         mate_take(2, (D,))
         extract(H[2])
         pass_on(q)
-        take(2, F)
-        take(2, C)
-        take(2, N2)
+        take_end(2, F)
+        take_end(2, C)
+        take_end(2, N2)
         pass_on(H[2])
         take(1, D)
         mate_take(1, (D,))
         extract(H[1])
-        mate_take(2, (F, C, N2))
+        mate_take_end(2, (F, C, N2))
     wait_diag(q)
     acc_lo[...] = product(q, 0, WS)
     acc_hi[...] = product(q, hi_lane, WS)
@@ -722,8 +736,8 @@
 
     @pl.when(outer)
     def _():
-        take(1, N2)
-        take(1, C)
+        take_end(1, N2)
+        take_end(1, C)
         pass_on(H[1])
     wait_diag(second)
     add_sides(second)
@@ -733,10 +747,10 @@
         take(0, D)
         mate_take(0, (D,))
         extract(H[0])
-        take(0, N2)
-        take(0, C)
-        take(1, F)
-        mate_take(1, (N2, C, F))
+        take_end(0, N2)
+        take_end(0, C)
+        take_end(1, F)
+        mate_take_end(1, (N2, C, F))
         wait_diag(H[1])
         add_sides(H[1])
     pass_on(H[0])
@@ -784,18 +798,18 @@
     def _():
         for p in (M1, M2):
             take(0, p)
+        put(slice(0, mid_lane), acc_lo)
+        put(slice(mid_lane + WM, R), acc_hi, mid_lane + WM - hi_lane)
         mate_take(0, (M1, M2))
         add_middle(H[0])
-        put(slice(0, mid_lane), acc_lo)
         put(slice(mid_lane, mid_lane + WM), acc_mid)
-        put(slice(mid_lane + WM, R), acc_hi, mid_lane + WM - hi_lane)
 
     lanes_lo = mid_lane, up_to(R // 2 + pad, 128)
     lanes_hi = (R // 2 - pad) // 128 * 128, mid_lane + WM
 
     @pl.when(outer)
     def _():
-        mate_take(0, (N2, C))
+        mate_take_end(0, (N2, C))
         wait_diag(H[0])
         for end, acc, begin, (first_mid, last_mid) in ((0, acc_lo, 0, lanes_lo), (3, acc_hi, hi_lane, lanes_hi)):
             @pl.when(q == end)
@@ -816,10 +830,10 @@
                 acc[...] += product(H[0], begin, WS)
                 put(slice(begin, begin + WS), acc)
         place = lax.broadcasted_iota(jnp.int32, (share, WM), 1) + mid_lane
-        first_lane = half + pad + jnp.where(upper, 0, 128)
-        last_lane = R // 2 + pad + jnp.where(upper, 128, 256)
-        inside = ((place >= first_lane) & (place < half + pad + 256)
-                  | (place >= R // 2 + pad) & (place < last_lane))
+        low_first = half + pad + jnp.where(upper, 0, share)
+        high_first = R // 2 + jnp.where(upper, 0, pad)
+        inside = ((place >= low_first) & (place < low_first + jnp.where(upper, 256, 128))
+                  | (place >= high_first) & (place < high_first + jnp.where(upper, 128, 256)))
         for d in (l, lx, ly, ld):
             wait_tile(d)
             placed = lax.dot_general(tile_recv[d], place_ref[...], (((1,), (0,)), ((), ())),
@@ -837,7 +851,7 @@
 
     @pl.when(inner)
     def _():
-        sent(zbuf.at[0, pl.ds(0, size[F] + size[C] + size[N2]), :], own_out)
+        sent(zbuf.at[0, pl.ds(0, size[F] + narrow + size[N2]), :], own_out)
         sent(zbuf.at[pl.ds(0, 2), pl.ds(0, size[D] - RAW), :], first_send)
         sent(raw, raw_send)
         sent(zbuf.at[pl.ds(0, 2), pl.ds(0, far), :], out_send)
@@ -884,12 +898,12 @@
             pltpu.VMEM((L * SP, WM), jnp.float32),
             pltpu.VMEM((2, L, 2, SP, 128), jnp.bfloat16),
             pltpu.VMEM((L, SP, 512), jnp.bfloat16),
-            pltpu.VMEM((up_to(share, 8), 128), jnp.bfloat16),
+            pltpu.VMEM((2, up_to(share, 8), 128), jnp.bfloat16),
             pltpu.VMEM((512, WM), jnp.bfloat16),
             pltpu.VMEM((R, 128), jnp.float32),
             pltpu.VMEM((B, 2, R), jnp.float32),
             pltpu.VMEM((R, T), jnp.float32),
-            pltpu.VMEM((2, (R - high) // 32 * 16, T), jnp.float32),
+            pltpu.VMEM((2, (R - high) * 7 // 256 * 16, T), jnp.float32),
             dma((B, 7)), dma, dma, dma, dma, dma, dma, dma, dma((2,)), dma,
             dma((B, 2)), dma, dma((B // 2,)), dma, dma((L,)), dma,
             dma, dma, dma((R // largest_tile(R, 352),)),

time: 58 us -> 57.3 us (0.988)
  Pallas kernels: 56.4 us -> 55.7 us
    pallas_call x1, Pallas kernels: 56.4 us -> 55.7 us  [line_call(): pl.pallas_call(functools.partial(line_kernel, L, B), out_shape=jax.ShapeD...]
where the time goes in v11:
time: 57.3 us; the launch traced here: 57.1 us
  Pallas kernels  55.7 us (97%)
  local copies, waits for them, and re-layouts  1.43 us (2%)
    pallas_call x1, Pallas kernels, line_call(): pl.pallas_call(functools.partial(line_kernel, L, B), out_shape=jax.ShapeD...  55.7 us
    unnamed x1, local copies, waits for them, and re-layouts  1.43 us

profile of v11, /device:TPU:0, one launch (start us, length us, event | category | flops | bytes accessed | tf_op | source)
XLA Modules:
  0.0 57.1 jit_solution(17864482369658805899)
XLA Ops:
  0.0 55.7 %shard_map.17 = f32[132,4,1056]{2,1,0:T(4,128)S(1)} custom-call(f32[1056,384]{1,0:T(8,128)} %x_hbm.1), custom_call_target="tpu_custom_call" | custom-call | tf_op jit(solution)/shard_map/pallas_call | solution.py:888
  55.7 1.4 %copy.3 = f32[4,132,1056]{2,0,1:T(4,128)} copy(f32[4,132,1056]{2,0,1:T(4,128)S(1)} %bitcast.1) | data formatting | bytes 4460544

commit v12 on v11

--- a/solution.py
+++ b/solution.py
@@ -753,6 +753,10 @@
         mate_take_end(1, (N2, C, F))
         wait_diag(H[1])
         add_sides(H[1])
+    @pl.when(inner)
+    def _():
+        mate_take(3, (F, M1, M2))
+        add_rows(l, H[3])
     pass_on(H[0])
 
     @pl.when(inner)
@@ -760,13 +764,11 @@
         take(0, F, send_out)
         for p in (N1, N2):
             z_copy(b, p, own_in, in_nbr).start()
-        mate_take(3, (F, M1, M2))
         mate_take(0, (F,))
-        add_rows(l, H[3])
         add_rows(l, H[0])
+        pass_on(H[3])
         turn_tiles(l)
         start_tiles(l)
-        pass_on(H[3])
 
         @pl.loop(0, 2)
         def _(n):

time: 57.3 us -> 57.2 us (level)
  no operation moved by 1% of the time
where the time goes in v12:
time: 57.2 us; the launch traced here: 57.1 us
  Pallas kernels  55.6 us (97%)
  local copies, waits for them, and re-layouts  1.43 us (2%)
    pallas_call x1, Pallas kernels, line_call(): pl.pallas_call(functools.partial(line_kernel, L, B), out_shape=jax.ShapeD...  55.6 us
    unnamed x1, local copies, waits for them, and re-layouts  1.43 us

profile of v12, /device:TPU:0, one launch (start us, length us, event | category | flops | bytes accessed | tf_op | source)
XLA Modules:
  0.0 57.1 jit_solution(6097472204375009083)
XLA Ops:
  0.0 55.6 %shard_map.17 = f32[132,4,1056]{2,1,0:T(4,128)S(1)} custom-call(f32[1056,384]{1,0:T(8,128)} %x_hbm.1), custom_call_target="tpu_custom_call" | custom-call | tf_op jit(solution)/shard_map/pallas_call | solution.py:890
  55.6 1.4 %copy.3 = f32[4,132,1056]{2,0,1:T(4,128)} copy(f32[4,132,1056]{2,0,1:T(4,128)S(1)} %bitcast.1) | data formatting | bytes 4460544

commit v13 on v12

--- a/solution.py
+++ b/solution.py
@@ -766,15 +766,18 @@
             z_copy(b, p, own_in, in_nbr).start()
         mate_take(0, (F,))
         add_rows(l, H[0])
-        pass_on(H[3])
         turn_tiles(l)
         start_tiles(l)
+
+        @pl.loop(0, 2)
+        def _(n):
+            add_rows(jnp.where(n == 0, lx, ly), H[0])
+        pass_on(H[3])
 
         @pl.loop(0, 2)
         def _(n):
             j = jnp.where(n == 0, lx, ly)
             add_rows(j, H[3])
-            add_rows(j, H[0])
             turn_tiles(j)
             start_tiles(j)
         for p in (N1, N2):

time: 57.2 us -> 57.3 us (level)
  no operation moved by 1% of the time
where the time goes in v13:
time: 57.3 us; the launch traced here: 57.1 us
  Pallas kernels  55.7 us (97%)
  local copies, waits for them, and re-layouts  1.43 us (2%)
    pallas_call x1, Pallas kernels, line_call(): pl.pallas_call(functools.partial(line_kernel, L, B), out_shape=jax.ShapeD...  55.7 us
    unnamed x1, local copies, waits for them, and re-layouts  1.43 us

profile of v13, /device:TPU:0, one launch (start us, length us, event | category | flops | bytes accessed | tf_op | source)
XLA Modules:
  0.0 57.1 jit_solution(13022806889248936521)
XLA Ops:
  0.0 55.7 %shard_map.17 = f32[132,4,1056]{2,1,0:T(4,128)S(1)} custom-call(f32[1056,384]{1,0:T(8,128)} %x_hbm.1), custom_call_target="tpu_custom_call" | custom-call | tf_op jit(solution)/shard_map/pallas_call | solution.py:893
  55.7 1.4 %copy.3 = f32[4,132,1056]{2,0,1:T(4,128)} copy(f32[4,132,1056]{2,0,1:T(4,128)S(1)} %bitcast.1) | data formatting | bytes 4460544

commit v14 on v13

--- a/solution.py
+++ b/solution.py
@@ -827,24 +827,29 @@
                     put(slice(last_mid, R), acc, last_mid - hi_lane)
                 else:
                     put(slice(0, first_mid), acc)
-        take(0, F)
-        mate_take(0, (F,))
-        for end, acc, begin in ((3, acc_lo, 0), (0, acc_hi, hi_lane)):
-            @pl.when(q == end)
-            def _():
-                acc[...] += product(H[0], begin, WS)
-                put(slice(begin, begin + WS), acc)
         place = lax.broadcasted_iota(jnp.int32, (share, WM), 1) + mid_lane
         low_first = half + pad + jnp.where(upper, 0, share)
         high_first = R // 2 + jnp.where(upper, 0, pad)
         inside = ((place >= low_first) & (place < low_first + jnp.where(upper, 256, 128))
                   | (place >= high_first) & (place < high_first + jnp.where(upper, 128, 256)))
-        for d in (l, lx, ly, ld):
+        def place_tile(d):
             wait_tile(d)
             placed = lax.dot_general(tile_recv[d], place_ref[...], (((1,), (0,)), ((), ())),
                                      preferred_element_type=jnp.float32)[:share]
             middle = pl.ds(mid_lane, WM)
             o_ref[:, d, middle] = jnp.where(inside, placed, o_ref[:, d, middle])
+
+        take(0, F)
+        place_tile(l)
+        place_tile(lx)
+        mate_take(0, (F,))
+        for end, acc, begin in ((3, acc_lo, 0), (0, acc_hi, hi_lane)):
+            @pl.when(q == end)
+            def _():
+                acc[...] += product(H[0], begin, WS)
+                put(slice(begin, begin + WS), acc)
+        place_tile(ly)
+        place_tile(ld)
 
     all_stats.wait_send()
     mate_own(b).wait_send()

time: 57.3 us -> 57.3 us (level)
  no operation moved by 1% of the time
where the time goes in v14:
time: 57.3 us; the launch traced here: 57.1 us
  Pallas kernels  55.7 us (97%)
  local copies, waits for them, and re-layouts  1.43 us (2%)
    pallas_call x1, Pallas kernels, line_call(): pl.pallas_call(functools.partial(line_kernel, L, B), out_shape=jax.ShapeD...  55.7 us
    unnamed x1, local copies, waits for them, and re-layouts  1.43 us

profile of v14, /device:TPU:0, one launch (start us, length us, event | category | flops | bytes accessed | tf_op | source)
XLA Modules:
  0.0 57.1 jit_solution(11304994221699098062)
XLA Ops:
  0.0 55.7 %shard_map.17 = f32[132,4,1056]{2,1,0:T(4,128)S(1)} custom-call(f32[1056,384]{1,0:T(8,128)} %x_hbm.1), custom_call_target="tpu_custom_call" | custom-call | tf_op jit(solution)/shard_map/pallas_call | solution.py:898
  55.7 1.4 %copy.3 = f32[4,132,1056]{2,0,1:T(4,128)} copy(f32[4,132,1056]{2,0,1:T(4,128)S(1)} %bitcast.1) | data formatting | bytes 4460544

commit v15 on v13

--- a/solution.py
+++ b/solution.py
@@ -347,7 +347,7 @@
     size = [edges[p + 1] - edges[p] for p in range(7)]
     narrow = size[C] // 2
     far = R - size[M2] - size[M1] - size[N1] - narrow
-    tile = largest_tile(R, 352)
+    tile = largest_tile(R, 528)
     RAW = raw.shape[1]
     WS = acc_lo.shape[1]
     hi_lane, mid_lane = R - WS, WS // 128 * 128
@@ -506,7 +506,7 @@
         part = shr.at[k, block, pl.ds(0, SR), :]
         return pltpu.make_async_remote_copy(
             src_ref=part, dst_ref=part, send_sem=shr_send,
-            recv_sem=shr_recv.at[k, way], device_id=(peer, b), device_id_type=MESH)
+            recv_sem=shr_recv.at[k // 2, way], device_id=(peer, b), device_id_type=MESH)
 
     SR = up_to(share, 8)
     cut = up_to(share // 2, 16)
@@ -537,13 +537,13 @@
             extract_one(place * 2 + core)
 
     def pass_on(place):
-        @pl.loop(0, 2)
-        def _(core):
-            k = place * 2 + core
-            share_copy(k, lx, lx, 0).wait_recv()
-            diag_copy(k, lx, ly, 0).start()
-            share_copy(k, ly, ly, 1).wait_recv()
-            diag_copy(k, ly, lx, 1).start()
+        for way, near, onward in ((0, lx, ly), (1, ly, lx)):
+            part = shr.at[pl.ds(place * 2, 2), near, pl.ds(0, SR), :]
+            pltpu.make_async_remote_copy(
+                src_ref=part, dst_ref=part, send_sem=shr_send, recv_sem=shr_recv.at[place, way],
+                device_id=(l, b), device_id_type=MESH).wait_recv()
+            for core in range(2):
+                diag_copy(place * 2 + core, near, onward, way).start()
 
     def wait_diag(place):
         part = shr.at[pl.ds(place * 2, 2), ld, pl.ds(0, SR), :]
@@ -910,8 +910,8 @@
             pltpu.VMEM((R, T), jnp.float32),
             pltpu.VMEM((2, (R - high) * 7 // 256 * 16, T), jnp.float32),
             dma((B, 7)), dma, dma, dma, dma, dma, dma, dma, dma((2,)), dma,
-            dma((B, 2)), dma, dma((B // 2,)), dma, dma((L,)), dma,
-            dma, dma, dma((R // largest_tile(R, 352),)),
+            dma((B // 2, 2)), dma, dma((B // 2,)), dma, dma((L,)), dma,
+            dma, dma, dma((R // largest_tile(R, 528),)),
         ],
         compiler_params=pltpu.CompilerParams(
             collective_id=0, has_side_effects=True, vmem_limit_bytes=34 * 1024 * 1024),

time: 57.3 us -> 57.2 us (level)
  no operation moved by 1% of the time
where the time goes in v15:
time: 57.2 us; the launch traced here: 57 us
  Pallas kernels  55.6 us (97%)
  local copies, waits for them, and re-layouts  1.43 us (2%)
    pallas_call x1, Pallas kernels, line_call(): pl.pallas_call(functools.partial(line_kernel, L, B), out_shape=jax.ShapeD...  55.6 us
    unnamed x1, local copies, waits for them, and re-layouts  1.43 us

profile of v15, /device:TPU:0, one launch (start us, length us, event | category | flops | bytes accessed | tf_op | source)
XLA Modules:
  0.0 57.0 jit_solution(8166045883677307124)
XLA Ops:
  0.0 55.6 %shard_map.17 = f32[132,4,1056]{2,1,0:T(4,128)S(1)} custom-call(f32[1056,384]{1,0:T(8,128)} %x_hbm.1), custom_call_target="tpu_custom_call" | custom-call | tf_op jit(solution)/shard_map/pallas_call | solution.py:893
  55.6 1.4 %copy.3 = f32[4,132,1056]{2,0,1:T(4,128)} copy(f32[4,132,1056]{2,0,1:T(4,128)S(1)} %bitcast.1) | data formatting | bytes 4460544
